TPU v7x, 32 devices: a whole 2x2x4 slice. The times are simulated.
32 devices in a mesh: gene: 4 (over x, core), cell: 8 (over z, y).
Axes of the slice: x: 2, y: 2, z: 4, core: 2. Of those that a mesh axis runs over, the one named last changes fastest.
Arguments:
- data: bfloat16 [19968, 4096], P('gene', 'cell'), may hold values from 0.049804688 to 5
- labels: int32 [32, 1], P('cell'), may hold values from 0 to 1; in each aligned block of 4 rows (0 to 3, 4 to 7, ...) at most 3 rows name the same one
- w_init: float32 [2, 19968], P(None, 'gene'), may hold values from 0.1 to 1
- h_init: float32 [2, 4096], P(None, 'cell'), may hold values from 0.1 to 2
Outputs:
- w_factor: float32 [2, 19968], P(None, 'gene')
- h_factor: float32 [2, 4096], P(None, 'cell')
- children: bfloat16 [19968, 8192], P('gene', 'cell')
Inputs may be any that keep to these rules, and one draw needn't show every extreme that they name: labels are 0 or 1; among the 4 blocks of one group of cells no label occurs more than 3 times, and some group reaches 3.
All inputs are finite; a program needn't handle non-finite values.
Results may differ from a plain program's by a relative error of at most 0.00057.
Values may be sent and summed in bfloat16 or wider, within the bound.
No kernel may reach another device: no remote copies, remote signals or barrier semaphores. Data moves between devices by JAX's collectives and lax.ppermute only.
A program may use at most 64 MiB of HBM per device.

v0:
```python
import jax
import jax.numpy as jnp
from jax import lax
from jax.sharding import PartitionSpec as P

ITERS = 2


FLOOR = 0.0001
GRAM_EPS = 1e-06


def swapped(block, axis, distance):
    count = lax.axis_size(axis)
    route = []
    for low in range(count):
        high = low | 1 << distance
        if high != low and high < count:
            route += [(low, high), (high, low)]
    return lax.ppermute(block, axis, route)


def update_rows(factor, numer, gram):
    first = jnp.maximum(
        factor[0]
        + (numer[0] - gram[0, 0] * factor[0] - gram[0, 1] * factor[1]) / (gram[0, 0] + GRAM_EPS),
        FLOOR,
    )
    second = jnp.maximum(
        factor[1]
        + (numer[1] - gram[1, 0] * first - gram[1, 1] * factor[1]) / (gram[1, 1] + GRAM_EPS),
        FLOOR,
    )
    return jnp.stack([first, second])


def body(data, labels, w_init, h_init):
    gene_rows = data.shape[0]
    cell_cols = data.shape[1]
    blocks_dev = cell_cols // 128
    w_factor = w_init
    h_factor = h_init
    for step in range(ITERS):
        w_round = w_factor.astype(jnp.bfloat16)
        w_part = jnp.dot(w_round, data, preferred_element_type=jnp.float32)
        wg_part = jnp.dot(w_round, w_round.T, preferred_element_type=jnp.float32)
        w_data, w_gram = lax.psum((w_part, wg_part), "gene")
        h_factor = update_rows(h_factor, w_data, w_gram)
        h_round = h_factor.astype(jnp.bfloat16)
        h_part = lax.dot_general(
            h_round, data, (((1,), (1,)), ((), ())), preferred_element_type=jnp.float32
        )
        hg_part = jnp.dot(h_round, h_round.T, preferred_element_type=jnp.float32)
        h_data, h_gram = lax.psum((h_part, hg_part), "cell")
        w_factor = update_rows(w_factor, h_data, h_gram)
    groups = lax.axis_size("cell")
    my_index = lax.axis_index("cell")
    half = (my_index >= groups // 2).astype(jnp.int32)
    bit_index = groups.bit_length() - 2
    labels_own = labels[:, 0]
    keep_own = labels_own == half
    blocks = data.reshape(gene_rows, blocks_dev, 128)
    zero = jnp.zeros((), jnp.bfloat16)
    own = jnp.where(keep_own[None, :, None], blocks, zero).reshape(gene_rows, cell_cols)
    most_out = blocks_dev - max(1, blocks_dev // 4)
    positions = jnp.arange(blocks_dev, dtype=jnp.int32)
    order = jnp.argsort(keep_own.astype(jnp.int32), stable=True)[:most_out]
    valid = jnp.logical_not(keep_own[order])
    select = ((order[:, None] == positions[None, :]) & valid[:, None]).astype(jnp.bfloat16)
    packed = jnp.einsum("mb,gbc->gmc", select, blocks, preferred_element_type=jnp.float32).astype(
        jnp.bfloat16
    )
    received = swapped(packed.reshape(gene_rows, most_out * 128), "cell", bit_index)
    every_label = lax.all_gather(labels, "cell", axis=0, tiled=True)
    partner = jnp.bitwise_xor(my_index, groups // 2)
    partner_labels = lax.dynamic_slice_in_dim(every_label[:, 0], partner * blocks_dev, blocks_dev)
    partner_keep = partner_labels == 1 - half
    partner_order = jnp.argsort(partner_keep.astype(jnp.int32), stable=True)[:most_out]
    partner_valid = jnp.logical_not(partner_keep[partner_order])
    placing = ((partner_order[:, None] == positions[None, :]) & partner_valid[:, None]).astype(
        jnp.bfloat16
    )
    spread = jnp.einsum(
        "mb,gmc->gbc",
        placing,
        received.reshape(gene_rows, most_out, 128),
        preferred_element_type=jnp.float32,
    )
    other = spread.astype(jnp.bfloat16).reshape(gene_rows, cell_cols)
    children = jnp.concatenate([own, other], axis=1)
    return (w_factor, h_factor, children)


def solution(mesh):
    placed = (P("gene", "cell"), P("cell", None), P(None, "gene"), P(None, "cell"))
    return jax.shard_map(
        body,
        mesh=mesh,
        in_specs=placed,
        out_specs=(P(None, "gene"), P(None, "cell"), P("gene", "cell")),
        check_vma=False,
    )
```

profile of v0, /device:TPU:0, one launch (start us, length us, event | category | flops | bytes accessed | tf_op | source)
XLA Modules:
  0.0 328.6 jit_solution(9795372820450521320)
XLA Ops:
  0.6 0.7 fusion.35
  1.3 0.7 sort.31
  2.1 0.6 gather_fusion
  2.7 9.5 %reshape.38 = bf16[4992,4,128]{2,1,0:T(4,128)(2,1)} reshape(bf16[4992,512]{1,0:T(8,128)(2,1)} %param.4) | data formatting | bytes 10223616 | tf_op jit(solution)/shard_map/reshape | solution.py:62
  12.2 7.6 %convert_bitcast_fusion = bf16[4992,3,128]{2,1,0:T(4,128)(2,1)} fusion(bf16[4992,4,128]{2,1,0:T(4,128)(2,1)} %reshape.38, s32[3]{0:T(128)S(1)} %get-tuple-element.50, pred[3]{0:T(512)(128)(4,1)S(1)} %not.14), kind=kOutput, calls=%fused_computation.4 | convolution fusion | flops 17252376 | bytes 8945679 | tf_op jit(solution)/shard_map/mb,gbc->gmc/dot_general | solution.py:70
  19.8 8.5 %copy.7 = bf16[4992,3,128]{0,2,1:T(8,128)(2,1)} copy(bf16[4992,3,128]{2,1,0:T(4,128)(2,1)} %convert_bitcast_fusion) | data formatting | bytes 7667712 | tf_op jit(solution)/shard_map/convert_element_type | solution.py:70
  28.3 4.1 %collective-permute-start = (bf16[4992,384]{0,1:T(8,128)(2,1)}, bf16[4992,384]{0,1:T(8,128)(2,1)}, u32[]{:S(2)}, u32[]{:S(2)}) collective-permute-start(bf16[4992,384]{0,1:T(8,128)(2,1)} %bitcast.55), channel_id=1, source_target_pairs={{0,4},{4,0},{1,5},{5,1},{2,6},{6,2},{3,7},{7,3},{8,12},{12,8},{9,1... | collective-permute-start | bytes 11501576 | tf_op jit(solution)/shard_map/ppermute | solution.py:20
  32.4 0.0 copy-done
  32.4 0.1 fusion.8
  32.5 3.2 fusion.10
  35.7 6.4 %all-reduce.4 = (f32[2,512]{1,0:T(2,128)S(1)}, f32[2,2]{1,0:T(2,128)S(1)}) all-reduce(f32[2,512]{1,0:T(2,128)S(1)} %fusion.10, f32[2,2]{1,0:T(2,128)S(1)} %fusion.8), channel_id=1, replica_groups=mesh['gene'=4,'cell'=8] {'gene'}, use_global_device_ids=true, to_apply=%region_0.0 | all-reduce | flops 1028 | bytes 8224 | tf_op jit(solution)/shard_map/psum | solution.py:47
  42.1 0.7 fusion.49
  44.0 0.0 copy-done.2
  44.0 1.3 fusion.42
  45.3 1.3 fusion.44
  46.6 0.1 fusion.51
  46.8 3.9 %fusion.50 = f32[2,4992]{1,0:T(2,128)S(1)} fusion(bf16[2,512]{1,0:T(2,128)(2,1)S(1)} %pad_maximum_fusion.4, bf16[4992,512]{1,0:T(8,128)(2,1)} %param.4), kind=kOutput, calls=%fused_computation.79 | convolution fusion | flops 10223616 | bytes 5153792 | tf_op jit(solution)/shard_map/dot_general | solution.py:50
  50.7 170.9 %all-reduce.2 = (f32[2,4992]{1,0:T(2,128)S(1)}, f32[2,2]{1,0:T(2,128)S(1)}) all-reduce(f32[2,4992]{1,0:T(2,128)S(1)} %fusion.50, f32[2,2]{1,0:T(2,128)S(1)} %fusion.51), channel_id=1, replica_groups=mesh['gene'=4,'cell'=8] {'cell'}, use_global_device_ids=true, to_apply=%region_2.0 | all-reduce | flops 9988 | bytes 79904 | tf_op jit(solution)/shard_map/psum | solution.py:54
  221.6 0.7 fusion.48
  223.5 1.3 fusion.38
  224.8 1.4 fusion.40
  226.2 0.1 pad_maximum_fusion.2
  226.2 0.1 fusion.53
  226.4 3.2 fusion.52
  229.6 0.6 dynamic-slice.1
  230.9 0.1 bitcast_dynamic-update-slice_fusion
  231.0 11.5 %all-reduce = s32[32]{0:T(128)S(1)} all-reduce(s32[32]{0:T(128)S(1)} %bitcast_dynamic-update-slice_fusion), channel_id=1, replica_groups=mesh['gene'=4,'cell'=8] {'cell'}, use_global_device_ids=true, to_apply=%add | all-reduce | flops 32 | bytes 256
  242.5 0.1 fusion.34
  242.6 0.7 sort.32
  243.4 5.7 %all-reduce.3 = (f32[2,512]{1,0:T(2,128)S(1)}, f32[2,2]{1,0:T(2,128)S(1)}) all-reduce(f32[2,512]{1,0:T(2,128)S(1)} %fusion.52, f32[2,2]{1,0:T(2,128)S(1)} %fusion.53), channel_id=1, replica_groups=mesh['gene'=4,'cell'=8] {'gene'}, use_global_device_ids=true, to_apply=%region_4.0 | all-reduce | flops 1028 | bytes 8224 | tf_op jit(solution)/shard_map/psum | solution.py:47
  249.1 0.7 fusion.47
  251.0 2.6 fusion.25
  253.6 0.0 copy-start.1
  253.6 0.1 fusion.30
  253.7 0.6 gather_fusion.1
  254.3 3.9 %fusion.32 = f32[2,4992]{1,0:T(2,128)S(1)} fusion(bf16[4992,512]{1,0:T(8,128)(2,1)} %param.4, f32[2,512]{1,0:T(2,128)S(1)} %pad_maximum_fusion.3), kind=kOutput, calls=%fused_computation.65 | convolution fusion | flops 10224640 | bytes 5155840 | tf_op jit(solution)/shard_map/dot_general | solution.py:50
  258.2 35.3 %all-reduce.1 = (f32[2,4992]{1,0:T(2,128)S(1)}, f32[2,2]{1,0:T(2,128)S(1)}) all-reduce(f32[2,4992]{1,0:T(2,128)S(1)} %fusion.32, f32[2,2]{1,0:T(2,128)S(1)} %fusion.30), channel_id=1, replica_groups=mesh['gene'=4,'cell'=8] {'cell'}, use_global_device_ids=true, to_apply=%region_6.0 | all-reduce | flops 9988 | bytes 79904 | tf_op jit(solution)/shard_map/psum | solution.py:54
  293.5 0.7 fusion.46
  295.5 0.1 broadcast_bitcast_fusion
  295.6 2.6 fusion.7
  298.2 0.7 pad_maximum_fusion.1
  298.9 5.0 %broadcast_select_fusion = bf16[4992,512]{1,0:T(8,128)(2,1)} fusion(bf16[4992,512]{1,0:T(8,128)(2,1)} %param.4, pred[512]{0:T(512)(128)(4,1)S(1)} %broadcast_bitcast_fusion), kind=kLoop, calls=%fused_computation.5 | loop fusion | flops 2555904 | bytes 10224128 | tf_op jit(solution)/shard_map/jit(_where)/select_n | solution.py:64
  303.9 0.0 collective-permute-done
  303.9 8.6 %copy.8 = bf16[4992,3,128]{2,1,0:T(4,128)(2,1)} copy(bf16[4992,3,128]{0,2,1:T(8,128)(2,1)} %bitcast.21) | data formatting | bytes 7667712 | tf_op jit(solution)/shard_map/reshape | solution.py:86
  312.5 7.6 %convolution_convert_fusion = bf16[4992,128,4]{1,2,0:T(4,128)(2,1)} fusion(bf16[4992,3,128]{2,1,0:T(4,128)(2,1)} %copy.8, s32[3]{0:T(128)S(1)} %get-tuple-element.48, pred[3]{0:T(512)(128)(4,1)S(1)} %not.15), kind=kOutput, calls=%fused_computation.6 | convolution fusion | flops 17891352 | bytes 8945679 | tf_op jit(solution)/shard_map/mb,gmc->gbc/dot_general | solution.py:83
  320.1 3.5 %copy.11 = bf16[624,8,4,128]{3,1,2,0:T(8,128)(2,1)S(1)} copy(bf16[624,8,4,128]{3,2,1,0:T(4,128)(2,1)} %bitcast.54) | data formatting | bytes 10223616
  323.6 0.2 slice-done.1
  323.8 4.8 %pad_maximum_fusion = bf16[4992,1024]{1,0:T(8,128)(2,1)} fusion(bf16[4992,512]{1,0:T(8,128)(2,1)S(1)} %bitcast.53, bf16[4992,512]{1,0:T(8,128)(2,1)S(1)} %bitcast.52), kind=kLoop, calls=%fused_computation.2 | loop fusion | flops 20447232 | bytes 20447232 | tf_op jit(solution)/shard_map/concatenate | solution.py:90
  (22 shorter events, 0.1 us)
Async XLA Ops:
  19.8 12.6 %copy-start = (f32[2,4992]{1,0:T(2,128)S(1)}, f32[2,4992]{1,0:T(2,128)}, u32[]{:S(2)}) copy-start(f32[2,4992]{1,0:T(2,128)} %param.6) | copy-start | bytes 119812
  19.8 24.2 %copy-start.2 = (f32[2,512]{1,0:T(2,128)S(1)}, f32[2,512]{1,0:T(2,128)}, u32[]{:S(2)}) copy-start(f32[2,512]{1,0:T(2,128)} %param.7) | copy-start | bytes 12292
  28.3 275.6 %collective-permute-start = (bf16[4992,384]{0,1:T(8,128)(2,1)}, bf16[4992,384]{0,1:T(8,128)(2,1)}, u32[]{:S(2)}, u32[]{:S(2)}) collective-permute-start(bf16[4992,384]{0,1:T(8,128)(2,1)} %bitcast.55), channel_id=1, source_target_pairs={{0,4},{4,0},{1,5},{5,1},{2,6},{6,2},{3,7},{7,3},{8,12},{12,8},{9,1... | collective-permute-start | bytes 11501576 | tf_op jit(solution)/shard_map/ppermute | solution.py:20
  46.8 182.9 %copy-start.4 = (u32[32]{0:T(128)S(1)}, u32[32]{0:T(128)}, u32[]{:S(2)}) copy-start(u32[32]{0:T(128)} %constant.25) | copy-start | bytes 388
  46.8 184.1 %copy-start.3 = (s32[4,1]{0,1:T(1,128)S(1)}, s32[4,1]{0,1:T(1,128)}, u32[]{:S(2)}) copy-start(s32[4,1]{0,1:T(1,128)} %param.5) | copy-start | bytes 52
  253.6 50.3 %copy-start.1 = (f32[2,512]{1,0:T(2,128)}, f32[2,512]{1,0:T(2,128)S(1)}, u32[]{:S(2)}) copy-start(f32[2,512]{1,0:T(2,128)S(1)} %pad_maximum_fusion.3) | copy-start | bytes 12292
  312.5 11.1 %slice-start = ((s8[5111808]{0:T(1024)(128)(4,1)}), s8[917504]{0:T(1024)(128)(4,1)S(1)}, s32[]{:S(2)}) async-start(s8[5111808]{0:T(1024)(128)(4,1)} %bitcast.51), calls=%async_computation | async-start | bytes 1835008
  320.1 3.7 %slice-start.1 = ((s8[5111808]{0:T(1024)(128)(4,1)}), s8[4194304]{0:T(1024)(128)(4,1)S(1)}, s32[]{:S(2)}) async-start(s8[5111808]{0:T(1024)(128)(4,1)} %bitcast.51), calls=%async_computation.1 | async-start | bytes 8388608
where the time goes:
time: 330 us; the launch traced here: 329 us
  blocking collectives  230 us (70%)
  local copies, waits for them, and re-layouts  35.1 us (11%)
  matrix products  29.9 us (9%)
  other arithmetic  23.2 us (7%)
  between operations  6.41 us (2%)
  starting transfers between devices  4.06 us (1%)
    psum x2, blocking collectives, body(): h_data, h_gram = lax.psum((h_part, hg_part), 'cell')  206 us
    psum x2, blocking collectives, body(): w_data, w_gram = lax.psum((w_part, wg_part), 'gene')  12.1 us
    unnamed x1, blocking collectives  11.5 us
    reshape x1, local copies, waits for them, and re-layouts, body(): blocks = data.reshape(gene_rows, blocks_dev, 128)  9.53 us
    reshape x1, local copies, waits for them, and re-layouts, body(): received.reshape(gene_rows, most_out, 128)  8.57 us
    convert_element_type x1, local copies, waits for them, and re-layouts, body(): jnp.einsum('mb,gbc->gmc', select, blocks, preferred_element_type=jnp.floa...  8.49 us
    dot_general x2, matrix products, body(): lax.dot_general(h_round, data, (((1,), (1,)), ((), ())), preferred_elemen...  7.81 us
    dot_general x1, matrix products, body(): jnp.einsum('mb,gmc->gbc', placing, received.reshape(gene_rows, most_out,...  7.61 us
  transfers between devices with their start and end apart: 1, of which 0 were waited for; matrix products, arithmetic and copies ran while one was open for 11% of the time, Pallas kernels for 0%

commit v1 on v0

v1 whole, which is shorter than its diff:
```python
import functools

import jax
import jax.numpy as jnp
from jax import lax
from jax.experimental import pallas as pl
from jax.experimental.pallas import tpu as pltpu
from jax.sharding import PartitionSpec as P

ITERS = 2
BLOCK = 128

FLOOR = 0.0001
GRAM_EPS = 1e-06


def flipped(x, axis, mask):
    count = lax.axis_size(axis)
    return lax.ppermute(x, axis, [(i, i ^ mask) for i in range(count)])


def all_sum(x, axis):
    count = lax.axis_size(axis)
    if count & (count - 1):
        return lax.psum(x, axis)
    bit = count
    while bit > 1:
        high, low = bit >> 1, bit >> 2
        if low:
            x = (x + flipped(x, axis, low)) + (flipped(x, axis, high) + flipped(x, axis, high | low))
        else:
            x = x + flipped(x, axis, high)
        bit = low or high
        if not low:
            break
    return x


def update_rows(factor, numer, gram):
    first = jnp.maximum(
        factor[0]
        + (numer[0] - gram[0, 0] * factor[0] - gram[0, 1] * factor[1]) / (gram[0, 0] + GRAM_EPS),
        FLOOR,
    )
    second = jnp.maximum(
        factor[1]
        + (numer[1] - gram[1, 0] * first - gram[1, 1] * factor[1]) / (gram[1, 1] + GRAM_EPS),
        FLOOR,
    )
    return jnp.stack([first, second])


def nth(flags, blocks, turn):
    leaving = sum(1 - flags[b] for b in range(blocks))
    found, low, high = 0, 0, leaving
    for b in range(blocks):
        rank = jnp.where(flags[b] > 0, high, low)
        found = found + jnp.where(rank == turn, b, 0)
        low, high = low + 1 - flags[b], high + flags[b]
    return found


def pack_kernel(flags, data, after, out):
    out[0] = data[...]


def pack(flags, data, after, first, count, parts):
    rows = data.shape[0] // parts
    blocks = data.shape[1] // BLOCK
    return pl.pallas_call(
        pack_kernel,
        grid_spec=pltpu.PrefetchScalarGridSpec(
            num_scalar_prefetch=1,
            grid=(count,),
            in_specs=[
                pl.BlockSpec(
                    (rows, BLOCK), lambda i, f: ((first + i) % parts, nth(f, blocks, (first + i) // parts))
                ),
                pl.BlockSpec(memory_space=pl.ANY),
            ],
            out_specs=pl.BlockSpec((1, rows, BLOCK), lambda i, f: (i, 0, 0)),
        ),
        out_shape=jax.ShapeDtypeStruct((count, rows, BLOCK), data.dtype),
        cost_estimate=pl.CostEstimate(flops=0, bytes_accessed=4 * count * rows * BLOCK, transcendentals=0),
    )(flags, data, after)


def keep_kernel(blocks, flags, data, after, out):
    for b in range(blocks):
        cols = slice(b * BLOCK, (b + 1) * BLOCK)
        kept = flags[b] > 0
        out[:, cols] = jnp.where(kept, data[:, cols], jnp.zeros_like(data[:, cols]))
    out[:, blocks * BLOCK :] = jnp.zeros((out.shape[0], blocks * BLOCK), out.dtype)


def keep(flags, data, after):
    rows, cols = data.shape
    tile = next(t for t in (624, 312, 208, 16, rows) if rows % t == 0)
    return pl.pallas_call(
        functools.partial(keep_kernel, cols // BLOCK),
        grid_spec=pltpu.PrefetchScalarGridSpec(
            num_scalar_prefetch=1,
            grid=(rows // tile,),
            in_specs=[
                pl.BlockSpec((tile, cols), lambda i, f: (i, 0)),
                pl.BlockSpec(memory_space=pl.ANY),
            ],
            out_specs=pl.BlockSpec((tile, 2 * cols), lambda i, f: (i, 0)),
        ),
        out_shape=jax.ShapeDtypeStruct((rows, 2 * cols), data.dtype),
        cost_estimate=pl.CostEstimate(flops=0, bytes_accessed=6 * rows * cols, transcendentals=0),
        name="keep",
    )(flags, data, after)


def place_kernel(first, parts, blocks, flags, got, held, out):
    sent = sum(1 - flags[b] for b in range(blocks))
    valid = (first + pl.program_id(0)) // parts < sent
    out[...] = jnp.where(valid, got[0], jnp.zeros_like(got[0]))


def place(flags, got, held, first, parts):
    _, cols = held.shape
    blocks = cols // BLOCK // 2
    count, tile, _ = got.shape
    return pl.pallas_call(
        functools.partial(place_kernel, first, parts, blocks),
        grid_spec=pltpu.PrefetchScalarGridSpec(
            num_scalar_prefetch=1,
            grid=(count,),
            in_specs=[
                pl.BlockSpec((1, tile, BLOCK), lambda i, f: (i, 0, 0)),
                pl.BlockSpec(memory_space=pl.ANY),
            ],
            out_specs=pl.BlockSpec(
                (tile, BLOCK),
                lambda i, f: ((first + i) % parts, blocks + nth(f, blocks, (first + i) // parts)),
            ),
        ),
        out_shape=jax.ShapeDtypeStruct(held.shape, held.dtype),
        input_output_aliases={2: 0},
        cost_estimate=pl.CostEstimate(flops=0, bytes_accessed=4 * count * tile * BLOCK, transcendentals=0),
    )(flags, got, held)


def with_gram(part, factor):
    gram = jnp.dot(factor, factor.T, preferred_element_type=jnp.float32)
    return jnp.concatenate([part, jnp.pad(gram, ((0, 0), (0, BLOCK - factor.shape[0])))], axis=1)


def steps(data, labels, w_init, h_init):
    rows, cols = data.shape
    blocks = cols // BLOCK
    groups = lax.axis_size("cell")
    across = groups // 2
    half = (lax.axis_index("cell") >= across).astype(jnp.int32)
    most = blocks - max(1, blocks // 4)
    parts = next(p for p in (4, 2, 1) if rows % (16 * p) == 0)
    flags = (labels[:, 0] == half).astype(jnp.int32)
    always = max(1, most - 1) * parts
    cuts = [0, always // 4, always * 5 // 8, always]
    packed = [
        pack(flags, data, w_init, cuts[i], cuts[i + 1] - cuts[i], parts) for i in range(len(cuts) - 1)
    ]

    def send(i):
        return flipped(packed[i], "cell", across)

    got = [send(0)]
    flags_in = flipped(flags, "cell", across)
    w_factor = w_init
    h_factor = h_init
    for step in range(ITERS):
        w_round = w_factor.astype(jnp.bfloat16)
        w_part = jnp.dot(w_round, data, preferred_element_type=jnp.float32)
        w_sum = all_sum(with_gram(w_part, w_round), "gene")
        h_factor = update_rows(h_factor, w_sum[:, :cols], w_sum[:, cols : cols + 2])
        h_round = h_factor.astype(jnp.bfloat16)
        h_part = lax.dot_general(
            h_round, data, (((1,), (1,)), ((), ())), preferred_element_type=jnp.float32
        )
        h_sum = all_sum(with_gram(h_part, h_round), "cell")
        if step + 1 < len(cuts) - 1:
            got.append(send(step + 1))
        w_factor = update_rows(w_factor, h_sum[:, :rows], h_sum[:, rows : rows + 2])
    last = pack(flags, data, w_factor, always, most * parts - always, parts)
    needed = (blocks - jnp.minimum(jnp.sum(flags), jnp.sum(flags_in))) * parts > always
    late = lax.cond(needed, lambda x: flipped(x, "cell", across), lambda x: x, last)
    children = keep(flags, data, w_factor)
    for i, x in enumerate(got):
        children = place(flags_in, x, children, cuts[i], parts)
    children = place(flags_in, late, children, always, parts)
    return (w_factor, h_factor, children)


def solution(mesh):
    placed = (P("gene", "cell"), P("cell", None), P(None, "gene"), P(None, "cell"))
    return jax.shard_map(
        steps,
        mesh=mesh,
        in_specs=placed,
        out_specs=(P(None, "gene"), P(None, "cell"), P("gene", "cell")),
        check_vma=False,
    )
```

time: 330 us -> 211 us (0.64)
  the two profiles are of different devices: /device:TPU:0 before, /device:TPU:28 now
where the time goes in v1:
time: 211 us; the launch traced here: 210 us
  waiting for transfers between devices  116 us (55%)
  Pallas kernels  34.5 us (16%)
  starting transfers between devices  21 us (10%)
  matrix products  15.6 us (7%)
  other arithmetic  12.6 us (6%)
  between operations  7.04 us (3%)
  local copies, waits for them, and re-layouts  3.41 us (2%)
    ppermute x19, waiting for transfers between devices, flipped(): return lax.ppermute(x, axis, [(i, i ^ mask) for i in range(count)])  116 us
    ppermute x19, starting transfers between devices, flipped(): return lax.ppermute(x, axis, [(i, i ^ mask) for i in range(count)])  21 us
    pallas_call x4, Pallas kernels, pack(): pl.pallas_call(pack_kernel, grid_spec=pltpu.PrefetchScalarGridSpec(num_sc...  12.9 us
    pallas_call x4, Pallas kernels, place(): pl.pallas_call(functools.partial(place_kernel, first, parts, blocks), gri...  12.5 us
    pallas_call x1, Pallas kernels, keep(): pl.pallas_call(functools.partial(keep_kernel, cols // BLOCK), grid_spec=p...  9.06 us
    dot_general x2, matrix products, steps(): lax.dot_general(h_round, data, (((1,), (1,)), ((), ())), preferred_elemen...  7.78 us
    dot_general x2, matrix products, steps(): w_part = jnp.dot(w_round, data, preferred_element_type=jnp.float32)  6.47 us
    another operation x4, other arithmetic  5.17 us
  transfers between devices with their start and end apart: 19, of which 9 were waited for; matrix products, arithmetic and copies ran while one was open for 3% of the time, Pallas kernels for 13%

profile of v1, /device:TPU:28, one launch (start us, length us, event | category | flops | bytes accessed | tf_op | source)
XLA Modules:
  0.0 210.1 jit_solution(6436945536719430840)
XLA Ops:
  0.6 1.0 fusion.8
  1.6 3.3 %fusion.10 = f32[2,512]{1,0:T(2,128)S(1)} fusion(bf16[4992,512]{1,0:T(8,128)(2,1)} %data.9, f32[2,4992]{1,0:T(2,128)} %after.5), kind=kOutput, calls=%fused_computation.25 | convolution fusion | flops 10233600 | bytes 5155840 | tf_op jit(solution)/shard_map/dot_general | solution.py:175
  4.9 1.6 collective-permute-start.2
  6.8 1.8 collective-permute-done.2
  8.6 0.9 collective-permute-done.3
  9.5 0.6 fusion.39
  11.4 1.2 fusion.32
  12.6 1.3 fusion.34
  13.9 3.9 %fusion.40 = f32[2,4992]{1,0:T(2,128)S(1)} fusion(bf16[2,512]{1,0:T(2,128)(2,1)S(1)} %pad_maximum_fusion.3, bf16[4992,512]{1,0:T(8,128)(2,1)} %data.9), kind=kOutput, calls=%fused_computation.65 | convolution fusion | flops 10223616 | bytes 5153792 | tf_op jit(solution)/shard_map/dot_general | solution.py:179
  18.8 3.6 %collective-permute-start.6 = (f32[2,5120]{1,0:T(2,128)S(1)}, f32[2,5120]{1,0:T(2,128)S(1)}, u32[]{:S(2)}, u32[]{:S(2)}) collective-permute-start(f32[2,5120]{1,0:T(2,128)S(1)} %select_maximum_fusion.1), channel_id=1, source_target_pairs={{0,6},{1,7},{2,4},{3,5},{4,2},{5,3},{6,0},{7,1},{8,14},{9,15},{10,... | collective-permute-start | bytes 122888 | tf_op jit(solution)/shard_map/ppermute | solution.py:19
  22.5 2.6 %collective-permute-done.5 = f32[2,5120]{1,0:T(2,128)S(1)} collective-permute-done((f32[2,5120]{1,0:T(2,128)S(1)}, f32[2,5120]{1,0:T(2,128)S(1)}, u32[]{:S(2)}, u32[]{:S(2)}) %collective-permute-start.5) | collective-permute-done | bytes 40992 | tf_op jit(solution)/shard_map/ppermute | solution.py:19
  25.7 3.5 %collective-permute-done.7 = f32[2,5120]{1,0:T(2,128)S(1)} collective-permute-done((f32[2,5120]{1,0:T(2,128)S(1)}, f32[2,5120]{1,0:T(2,128)S(1)}, u32[]{:S(2)}, u32[]{:S(2)}) %collective-permute-start.7) | collective-permute-done | bytes 40992 | tf_op jit(solution)/shard_map/ppermute | solution.py:19
  29.2 0.6 fusion.37
  31.0 1.3 fusion.28
  32.3 1.4 fusion.30
  33.8 3.2 %fusion.42 = f32[2,512]{1,0:T(2,128)S(1)} fusion(bf16[2,4992]{1,0:T(2,128)(2,1)S(1)} %pad_maximum_fusion.1, bf16[4992,512]{1,0:T(8,128)(2,1)} %data.9), kind=kOutput, calls=%fused_computation.67 | convolution fusion | flops 10223616 | bytes 5135872 | tf_op jit(solution)/shard_map/dot_general | solution.py:175
  37.2 0.7 collective-permute-start.8
  37.8 1.5 collective-permute-start.9
  39.3 0.9 collective-permute-done.10
  40.2 1.2 collective-permute-done.9
  43.2 2.5 %fusion.19 = (f32[1,512]{1,0:T(1,128)S(1)}, f32[1,512]{1,0:T(1,128)S(1)}) fusion(f32[1,512]{1,0:T(1,128)S(1)} %get-tuple-element.19, f32[2,640]{1,0:T(2,128)S(1)} %add_add_fusion.2, f32[]{:T(128)S(6)} %add.138, f32[]{:T(128)} %bitcast.11, f32[]{:T(128)} %bitcast.10, f32[1,512]{1,0:T(1,128)S(1)} %get-tuple-element.17, f32[]{:T(128)S(6)} %add.136, f32[]{:T(128)} %bitcast.9, ...), kind=kLoop, calls=%fused_computation.50 | loop fusion | flops 7168 | bytes 12312 | tf_op jit(solution)/shard_map/max | solution.py:45
  45.8 3.9 %fusion.22 = f32[2,4992]{1,0:T(2,128)S(1)} fusion(bf16[4992,512]{1,0:T(8,128)(2,1)} %data.9, f32[2,512]{1,0:T(2,128)S(1)} %pad_maximum_fusion.2), kind=kOutput, calls=%fused_computation.53 | convolution fusion | flops 10224640 | bytes 5155840 | tf_op jit(solution)/shard_map/dot_general | solution.py:179
  49.9 1.1 collective-permute-start.11
  50.9 2.8 %collective-permute-start.12 = (f32[2,5120]{1,0:T(2,128)S(1)}, f32[2,5120]{1,0:T(2,128)S(1)}, u32[]{:S(2)}, u32[]{:S(2)}) collective-permute-start(f32[2,5120]{1,0:T(2,128)S(1)} %select_maximum_fusion), channel_id=1, source_target_pairs={{0,4},{1,5},{2,6},{3,7},{4,0},{5,1},{6,2},{7,3},{8,12},{9,13},{10,... | collective-permute-start | bytes 122888 | tf_op jit(solution)/shard_map/ppermute | solution.py:19
  53.7 0.6 collective-permute-start.13
  54.3 1.0 collective-permute-start.15
  55.3 2.5 %shard_map.70 = bf16[2,1248,128]{2,1,0:T(8,128)(2,1)} custom-call(s32[4]{0:T(128)} %copy-done.4, bf16[4992,512]{1,0:T(8,128)(2,1)} %data.9, f32[2,4992]{1,0:T(2,128)} %after.5), custom_call_target="tpu_custom_call" | custom-call | bytes 1277952 | tf_op jit(solution)/shard_map/pallas_call | solution.py:70
  57.9 2.0 collective-permute-start.18
  59.9 3.7 %shard_map.69 = bf16[3,1248,128]{2,1,0:T(8,128)(2,1)} custom-call(s32[4]{0:T(128)} %copy-done.4, bf16[4992,512]{1,0:T(8,128)(2,1)} %data.9, f32[2,4992]{1,0:T(2,128)} %after.5), custom_call_target="tpu_custom_call" | custom-call | bytes 1916928 | tf_op jit(solution)/shard_map/pallas_call | solution.py:70
  63.5 3.8 %shard_map.68 = bf16[3,1248,128]{2,1,0:T(8,128)(2,1)} custom-call(s32[4]{0:T(128)} %copy-done.4, bf16[4992,512]{1,0:T(8,128)(2,1)} %data.9, f32[2,4992]{1,0:T(2,128)} %after.5), custom_call_target="tpu_custom_call" | custom-call | bytes 1916928 | tf_op jit(solution)/shard_map/pallas_call | solution.py:70
  67.3 0.9 collective-permute-start.17
  68.3 2.0 collective-permute-start.16
  70.9 0.6 fusion.24
  71.5 0.6 reduce_sum.19
  73.5 0.9 collective-permute-done.14
  74.4 0.6 fusion.36
  76.2 2.6 %fusion.7 = (f32[1,4992]{1,0:T(1,128)S(1)}, f32[1,4992]{1,0:T(1,128)S(1)}) fusion(f32[1,4992]{1,0:T(1,128)S(1)} %get-tuple-element.15, f32[2,5120]{1,0:T(2,128)S(1)} %add.143, f32[]{:T(128)S(6)} %add.146, f32[]{:T(128)} %bitcast.15, f32[]{:T(128)} %bitcast.14, f32[1,4992]{1,0:T(1,128)S(1)} %get-tuple-element.13, f32[]{:T(128)S(6)} %add.144, f32[]{:T(128)} %bitcast.13, ...), kind=kLoop, calls=%fused_computation.22 | loop fusion | flops 69888 | bytes 119832 | tf_op jit(solution)/shard_map/max | solution.py:45
  78.9 0.7 pad_maximum_fusion.after
  79.5 9.1 %keep.1.held = bf16[4992,1024]{1,0:T(8,128)(2,1)} custom-call(s32[4]{0:T(128)} %copy-done.4, bf16[4992,512]{1,0:T(8,128)(2,1)} %data.9, f32[2,4992]{1,0:T(2,128)} %pad_maximum_fusion.after), custom_call_target="tpu_custom_call" | custom-call | bytes 15335424 | tf_op jit(solution)/shard_map/keep/pallas_call | solution.py:99
  88.6 2.9 %shard_map.67 = bf16[4,1248,128]{2,1,0:T(8,128)(2,1)S(1)} custom-call(s32[4]{0:T(128)} %copy-done.4, bf16[4992,512]{1,0:T(8,128)(2,1)} %data.9, f32[2,4992]{1,0:T(2,128)} %pad_maximum_fusion.after), custom_call_target="tpu_custom_call" | custom-call | bytes 2555904 | tf_op jit(solution)/shard_map/pallas_call | solution.py:70
  91.5 105.1 %conditional.1 = (bf16[4,1248,128]{2,1,0:T(8,128)(2,1)S(1)}) conditional(s32[]{:T(128)} %convert_element_type.29, bf16[4,1248,128]{2,1,0:T(8,128)(2,1)S(1)} %shard_map.67, bf16[4,1248,128]{2,1,0:T(8,128)(2,1)S(1)} %shard_map.67), branch_computations={%region_2.3_spmd, %region_3.4_spmd} | conditional | bytes 7667760 | solution.py:188
  91.5 1.0 collective-permute-start
  92.5 104.0 %collective-permute-done = bf16[4,1248,128]{2,1,0:T(8,128)(2,1)S(1)} collective-permute-done((bf16[4,1248,128]{2,1,0:T(8,128)(2,1)S(1)}, bf16[4,1248,128]{2,1,0:T(8,128)(2,1)S(1)}, u32[]{:S(2)}, u32[]{:S(2)}) %collective-permute-start) | collective-permute-done | bytes 1277984 | tf_op jit(solution)/shard_map/cond/branch_1_fun/ppermute | solution.py:19
  196.6 2.6 %shard_map.71.held = bf16[4992,1024]{1,0:T(8,128)(2,1)} custom-call(s32[4]{0:T(128)} %copy-done.6, bf16[2,1248,128]{2,1,0:T(8,128)(2,1)} %collective-permute-done.18.got, bf16[4992,1024]{1,0:T(8,128)(2,1)} %keep.1.held), custom_call_target="tpu_custom_call", output_to_operand_aliasing={{}: (2, {})} | custom-call | bytes 1277952 | tf_op jit(solution)/shard_map/pallas_call | solution.py:126
  199.2 0.9 copy-done.2
  200.1 3.8 %shard_map.72.held = bf16[4992,1024]{1,0:T(8,128)(2,1)} custom-call(s32[4]{0:T(128)} %copy-done.6, bf16[3,1248,128]{2,1,0:T(8,128)(2,1)} %copy-done.2, bf16[4992,1024]{1,0:T(8,128)(2,1)} %shard_map.71.held), custom_call_target="tpu_custom_call", output_to_operand_aliasing={{}: (2, {})} | custom-call | bytes 1916928 | tf_op jit(solution)/shard_map/pallas_call | solution.py:126
  203.9 3.8 %shard_map.73.held = bf16[4992,1024]{1,0:T(8,128)(2,1)} custom-call(s32[4]{0:T(128)} %copy-done.6, bf16[3,1248,128]{2,1,0:T(8,128)(2,1)} %collective-permute-done.16.got, bf16[4992,1024]{1,0:T(8,128)(2,1)} %shard_map.72.held), custom_call_target="tpu_custom_call", output_to_operand_aliasing={{}: (2, {})} | custom-call | bytes 1916928 | tf_op jit(solution)/shard_map/pallas_call | solution.py:126
  207.6 2.4 %shard_map.74 = bf16[4992,1024]{1,0:T(8,128)(2,1)} custom-call(s32[4]{0:T(128)} %copy-done.6, bf16[4,1248,128]{2,1,0:T(8,128)(2,1)S(1)} %get-tuple-element.36.got, bf16[4992,1024]{1,0:T(8,128)(2,1)} %shard_map.73.held), custom_call_target="tpu_custom_call", output_to_operand_aliasing={{}: (2, {})} | custom-call | bytes 2555904 | tf_op jit(solution)/shard_map/pallas_call | solution.py:126
  (52 shorter events, 3.8 us)
Async XLA Ops:
  0.6 10.7 %copy-start.5 = (f32[2,512]{1,0:T(2,128)S(1)}, f32[2,512]{1,0:T(2,128)}, u32[]{:S(2)}) copy-start(f32[2,512]{1,0:T(2,128)} %param.9) | copy-start | bytes 12292
  1.6 29.4 %copy-start = (f32[2,4992]{1,0:T(2,128)S(1)}, f32[2,4992]{1,0:T(2,128)}, u32[]{:S(2)}) copy-start(f32[2,4992]{1,0:T(2,128)} %after.5) | copy-start | bytes 119812
  4.9 1.9 collective-permute-start.1
  4.9 3.7 %collective-permute-start.2 = (f32[2,640]{1,0:T(2,128)S(1)}, f32[2,640]{1,0:T(2,128)S(1)}, u32[]{:S(2)}, u32[]{:S(2)}) collective-permute-start(f32[2,640]{1,0:T(2,128)S(1)} %select_maximum_fusion.3), channel_id=1, source_target_pairs={{0,16},{8,24},{16,0},{24,8},{1,17},{9,25},{17,1},{25,9},{2,18},{10... | collective-permute-start | bytes 15368 | tf_op jit(solution)/shard_map/ppermute | solution.py:19
  6.5 3.0 %collective-permute-start.3 = (f32[2,640]{1,0:T(2,128)S(1)}, f32[2,640]{1,0:T(2,128)S(1)}, u32[]{:S(2)}, u32[]{:S(2)}) collective-permute-start(f32[2,640]{1,0:T(2,128)S(1)} %select_maximum_fusion.3), channel_id=1, source_target_pairs={{0,24},{8,16},{16,8},{24,0},{1,25},{9,17},{17,9},{25,1},{2,26},{10... | collective-permute-start | bytes 15368 | tf_op jit(solution)/shard_map/ppermute | solution.py:19
  18.0 4.5 %collective-permute-start.4 = (f32[2,5120]{1,0:T(2,128)S(1)}, f32[2,5120]{1,0:T(2,128)S(1)}, u32[]{:S(2)}, u32[]{:S(2)}) collective-permute-start(f32[2,5120]{1,0:T(2,128)S(1)} %select_maximum_fusion.1), channel_id=1, source_target_pairs={{0,2},{1,3},{2,0},{3,1},{4,6},{5,7},{6,4},{7,5},{8,10},{9,11},{10,... | collective-permute-start | bytes 122888 | tf_op jit(solution)/shard_map/ppermute | solution.py:19
  18.5 6.6 %collective-permute-start.5 = (f32[2,5120]{1,0:T(2,128)S(1)}, f32[2,5120]{1,0:T(2,128)S(1)}, u32[]{:S(2)}, u32[]{:S(2)}) collective-permute-start(f32[2,5120]{1,0:T(2,128)S(1)} %select_maximum_fusion.1), channel_id=1, source_target_pairs={{0,4},{1,5},{2,6},{3,7},{4,0},{5,1},{6,2},{7,3},{8,12},{9,13},{10,... | collective-permute-start | bytes 122888 | tf_op jit(solution)/shard_map/ppermute | solution.py:19
  18.8 6.2 %collective-permute-start.6 = (f32[2,5120]{1,0:T(2,128)S(1)}, f32[2,5120]{1,0:T(2,128)S(1)}, u32[]{:S(2)}, u32[]{:S(2)}) collective-permute-start(f32[2,5120]{1,0:T(2,128)S(1)} %select_maximum_fusion.1), channel_id=1, source_target_pairs={{0,6},{1,7},{2,4},{3,5},{4,2},{5,3},{6,0},{7,1},{8,14},{9,15},{10,... | collective-permute-start | bytes 122888 | tf_op jit(solution)/shard_map/ppermute | solution.py:19
  25.1 4.1 %collective-permute-start.7 = (f32[2,5120]{1,0:T(2,128)S(1)}, f32[2,5120]{1,0:T(2,128)S(1)}, u32[]{:S(2)}, u32[]{:S(2)}) collective-permute-start(f32[2,5120]{1,0:T(2,128)S(1)} %add_add_fusion.1), channel_id=1, source_target_pairs={{0,1},{1,0},{2,3},{3,2},{4,5},{5,4},{6,7},{7,6},{8,9},{9,8},{10,11... | collective-permute-start | bytes 122888 | tf_op jit(solution)/shard_map/ppermute | solution.py:19
  33.7 20.6 %copy-start.7 = (s32[4,1]{0,1:T(1,128)S(1)}, s32[4,1]{0,1:T(1,128)}, u32[]{:S(2)}) copy-start(s32[4,1]{0,1:T(1,128)} %param.7) | copy-start | bytes 52
  37.1 3.1 %collective-permute-start.10 = (f32[2,640]{1,0:T(2,128)S(1)}, f32[2,640]{1,0:T(2,128)S(1)}, u32[]{:S(2)}, u32[]{:S(2)}) collective-permute-start(f32[2,640]{1,0:T(2,128)S(1)} %select_maximum_fusion.2), channel_id=1, source_target_pairs={{0,24},{8,16},{16,8},{24,0},{1,25},{9,17},{17,9},{25,1},{2,26},{10... | collective-permute-start | bytes 15368 | tf_op jit(solution)/shard_map/ppermute | solution.py:19
  37.2 3.0 %collective-permute-start.8 = (f32[2,640]{1,0:T(2,128)S(1)}, f32[2,640]{1,0:T(2,128)S(1)}, u32[]{:S(2)}, u32[]{:S(2)}) collective-permute-start(f32[2,640]{1,0:T(2,128)S(1)} %select_maximum_fusion.2), channel_id=1, source_target_pairs={{0,8},{8,0},{16,24},{24,16},{1,9},{9,1},{17,25},{25,17},{2,10},{10... | collective-permute-start | bytes 15368 | tf_op jit(solution)/shard_map/ppermute | solution.py:19
  37.8 3.6 %collective-permute-start.9 = (f32[2,640]{1,0:T(2,128)S(1)}, f32[2,640]{1,0:T(2,128)S(1)}, u32[]{:S(2)}, u32[]{:S(2)}) collective-permute-start(f32[2,640]{1,0:T(2,128)S(1)} %select_maximum_fusion.2), channel_id=1, source_target_pairs={{0,16},{8,24},{16,0},{24,8},{1,17},{9,25},{17,1},{25,9},{2,18},{10... | collective-permute-start | bytes 15368 | tf_op jit(solution)/shard_map/ppermute | solution.py:19
  45.8 12.1 %copy-start.3 = (f32[2,512]{1,0:T(2,128)}, f32[2,512]{1,0:T(2,128)S(1)}, u32[]{:S(2)}) copy-start(f32[2,512]{1,0:T(2,128)S(1)} %pad_maximum_fusion.2) | copy-start | bytes 12292
  49.9 17.5 %collective-permute-start.11 = (f32[2,5120]{1,0:T(2,128)S(1)}, f32[2,5120]{1,0:T(2,128)S(1)}, u32[]{:S(2)}, u32[]{:S(2)}) collective-permute-start(f32[2,5120]{1,0:T(2,128)S(1)} %select_maximum_fusion), channel_id=1, source_target_pairs={{0,2},{1,3},{2,0},{3,1},{4,6},{5,7},{6,4},{7,5},{8,10},{9,11},{10,... | collective-permute-start | bytes 122888 | tf_op jit(solution)/shard_map/ppermute | solution.py:19
  50.9 17.3 %collective-permute-start.12 = (f32[2,5120]{1,0:T(2,128)S(1)}, f32[2,5120]{1,0:T(2,128)S(1)}, u32[]{:S(2)}, u32[]{:S(2)}) collective-permute-start(f32[2,5120]{1,0:T(2,128)S(1)} %select_maximum_fusion), channel_id=1, source_target_pairs={{0,4},{1,5},{2,6},{3,7},{4,0},{5,1},{6,2},{7,3},{8,12},{9,13},{10,... | collective-permute-start | bytes 122888 | tf_op jit(solution)/shard_map/ppermute | solution.py:19
  53.7 16.6 %collective-permute-start.13 = (f32[2,5120]{1,0:T(2,128)S(1)}, f32[2,5120]{1,0:T(2,128)S(1)}, u32[]{:S(2)}, u32[]{:S(2)}) collective-permute-start(f32[2,5120]{1,0:T(2,128)S(1)} %select_maximum_fusion), channel_id=1, source_target_pairs={{0,6},{1,7},{2,4},{3,5},{4,2},{5,3},{6,0},{7,1},{8,14},{9,15},{10,... | collective-permute-start | bytes 122888 | tf_op jit(solution)/shard_map/ppermute | solution.py:19
  54.3 1.0 copy-start.4
  54.3 17.2 %collective-permute-start.15 = (s32[4]{0:T(128)S(1)}, s32[4]{0:T(128)S(1)}, u32[]{:S(2)}, u32[]{:S(2)}) collective-permute-start(s32[4]{0:T(128)S(1)} %fusion.25.flags), channel_id=1, source_target_pairs={{0,4},{1,5},{2,6},{3,7},{4,0},{5,1},{6,2},{7,3},{8,12},{9,13},{10,... | collective-permute-start | bytes 56 | tf_op jit(solution)/shard_map/ppermute | solution.py:19
  57.9 138.7 %collective-permute-start.18 = (bf16[2,1248,128]{2,1,0:T(8,128)(2,1)}, bf16[2,1248,128]{2,1,0:T(8,128)(2,1)}, u32[]{:S(2)}, u32[]{:S(2)}) collective-permute-start(bf16[2,1248,128]{2,1,0:T(8,128)(2,1)} %shard_map.70), channel_id=1, source_target_pairs={{0,4},{1,5},{2,6},{3,7},{4,0},{5,1},{6,2},{7,3},{8,12},{9,13},{10,... | collective-permute-start | bytes 1916936 | tf_op jit(solution)/shard_map/ppermute | solution.py:19
  63.5 3.8 %copy-start.1 = (bf16[3,1248,128]{2,1,0:T(8,128)(2,1)S(1)}, bf16[3,1248,128]{2,1,0:T(8,128)(2,1)}, u32[]{:S(2)}) copy-start(bf16[3,1248,128]{2,1,0:T(8,128)(2,1)} %shard_map.69) | copy-start | bytes 2875396
  67.3 131.9 %collective-permute-start.17 = (bf16[3,1248,128]{2,1,0:T(8,128)(2,1)S(1)}, bf16[3,1248,128]{2,1,0:T(8,128)(2,1)S(1)}, u32[]{:S(2)}, u32[]{:S(2)}) collective-permute-start(bf16[3,1248,128]{2,1,0:T(8,128)(2,1)S(1)} %copy-done.1), channel_id=1, source_target_pairs={{0,4},{1,5},{2,6},{3,7},{4,0},{5,1},{6,2},{7,3},{8,12},{9,13},{10,... | collective-permute-start | bytes 2875400 | tf_op jit(solution)/shard_map/ppermute | solution.py:19
  68.3 135.6 %collective-permute-start.16 = (bf16[3,1248,128]{2,1,0:T(8,128)(2,1)}, bf16[3,1248,128]{2,1,0:T(8,128)(2,1)}, u32[]{:S(2)}, u32[]{:S(2)}) collective-permute-start(bf16[3,1248,128]{2,1,0:T(8,128)(2,1)} %shard_map.68), channel_id=1, source_target_pairs={{0,4},{1,5},{2,6},{3,7},{4,0},{5,1},{6,2},{7,3},{8,12},{9,13},{10,... | collective-permute-start | bytes 2875400 | tf_op jit(solution)/shard_map/ppermute | solution.py:19
  70.3 4.1 %collective-permute-start.14 = (f32[2,5120]{1,0:T(2,128)S(1)}, f32[2,5120]{1,0:T(2,128)S(1)}, u32[]{:S(2)}, u32[]{:S(2)}) collective-permute-start(f32[2,5120]{1,0:T(2,128)S(1)} %add_add_fusion), channel_id=1, source_target_pairs={{0,1},{1,0},{2,3},{3,2},{4,5},{5,4},{6,7},{7,6},{8,9},{9,8},{10,11... | collective-permute-start | bytes 122888 | tf_op jit(solution)/shard_map/ppermute | solution.py:19
  71.5 17.1 %copy-start.6 = (s32[4]{0:T(128)}, s32[4]{0:T(128)S(1)}, u32[]{:S(2)}) copy-start(s32[4]{0:T(128)S(1)} %collective-permute-done.15.flags) | copy-start | bytes 52
  91.5 105.0 %collective-permute-start = (bf16[4,1248,128]{2,1,0:T(8,128)(2,1)S(1)}, bf16[4,1248,128]{2,1,0:T(8,128)(2,1)S(1)}, u32[]{:S(2)}, u32[]{:S(2)}) collective-permute-start(bf16[4,1248,128]{2,1,0:T(8,128)(2,1)S(1)} %param.1), channel_id=1, source_target_pairs={{0,4},{1,5},{2,6},{3,7},{4,0},{5,1},{6,2},{7,3},{8,12},{9,13},{10,... | collective-permute-start | bytes 3833864 | tf_op jit(solution)/shard_map/cond/branch_1_fun/ppermute | solution.py:19
  199.2 0.9 copy-start.2

commit v2 on v1

v2 whole, which is shorter than its diff:
```python
import functools

import jax
import jax.numpy as jnp
from jax import lax
from jax.experimental import pallas as pl
from jax.experimental.pallas import tpu as pltpu
from jax.sharding import PartitionSpec as P

ITERS = 2
BLOCK = 128

FLOOR = 0.0001
GRAM_EPS = 1e-06


def flipped(x, axis, mask):
    count = lax.axis_size(axis)
    return lax.ppermute(x, axis, [(i, i ^ mask) for i in range(count)])


def all_sum(x, axis):
    count = lax.axis_size(axis)
    if count & (count - 1):
        return lax.psum(x, axis)
    bit = count
    while bit > 1:
        high, low = bit >> 1, bit >> 2
        if low:
            x = (x + flipped(x, axis, low)) + (flipped(x, axis, high) + flipped(x, axis, high | low))
        else:
            x = x + flipped(x, axis, high)
        bit = low or high
        if not low:
            break
    return x


def update_rows(factor, numer, gram):
    first = jnp.maximum(
        factor[0]
        + (numer[0] - gram[0, 0] * factor[0] - gram[0, 1] * factor[1]) / (gram[0, 0] + GRAM_EPS),
        FLOOR,
    )
    second = jnp.maximum(
        factor[1]
        + (numer[1] - gram[1, 0] * first - gram[1, 1] * factor[1]) / (gram[1, 1] + GRAM_EPS),
        FLOOR,
    )
    return jnp.stack([first, second])


def runs(first, count, parts):
    found, at = [], first
    while at < first + count:
        size = min(parts - at % parts, first + count - at)
        found.append((at // parts, at % parts, size, at - first))
        at += size
    return found


def nth(leaves, turn):
    found, low, high = 0, 0, sum(leaves)
    for b, leave in enumerate(leaves):
        found = found + jnp.where(jnp.where(leave > 0, low, high) == turn, b, 0)
        low, high = low + leave, high + 1 - leave
    return found


def my_half():
    return (lax.axis_index("cell") >= lax.axis_size("cell") // 2).astype(jnp.int32)


def lanes(block):
    return pl.ds(pl.multiple_of(block * BLOCK, BLOCK), BLOCK)


def pack_kernel(first, parts, labels, data, out, sems):
    tile = data.shape[0] // parts
    half = my_half()
    leaves = [(labels[b] != half).astype(jnp.int32) for b in range(data.shape[1] // BLOCK)]
    copies = []
    for n, (block, at, size, before) in enumerate(runs(first, out.shape[0] // tile, parts)):
        copies.append(
            pltpu.make_async_copy(
                data.at[pl.ds(at * tile, size * tile), lanes(nth(leaves, block))],
                out.at[pl.ds(before * tile, size * tile), :],
                sems.at[n],
            )
        )
        copies[-1].start()
    for copy in copies:
        copy.wait()


def pack(labels, data, first, count, parts):
    shape = (count * data.shape[0] // parts, BLOCK)
    return pl.pallas_call(
        functools.partial(pack_kernel, first, parts),
        in_specs=[pl.BlockSpec(memory_space=pltpu.SMEM), pl.BlockSpec(memory_space=pl.ANY)],
        out_specs=pl.BlockSpec(memory_space=pltpu.VMEM),
        out_shape=jax.ShapeDtypeStruct(shape, data.dtype),
        scratch_shapes=[pltpu.SemaphoreType.DMA((len(runs(first, count, parts)),))],
        cost_estimate=pl.CostEstimate(flops=0, bytes_accessed=4 * shape[0] * BLOCK, transcendentals=0),
    )(labels, data)


def keep_kernel(blocks, labels, data, out):
    half = my_half()
    for b in range(blocks):
        cols = slice(b * BLOCK, (b + 1) * BLOCK)
        out[:, cols] = jnp.where(labels[b] == half, data[:, cols], jnp.zeros_like(data[:, cols]))
    out[:, blocks * BLOCK :] = jnp.zeros((out.shape[0], blocks * BLOCK), out.dtype)


def keep(labels, data):
    rows, cols = data.shape
    tile = next(t for t in (624, 312, 208, 16, rows) if rows % t == 0)
    return pl.pallas_call(
        functools.partial(keep_kernel, cols // BLOCK),
        grid=(rows // tile,),
        in_specs=[pl.BlockSpec(memory_space=pltpu.SMEM), pl.BlockSpec((tile, cols), lambda i: (i, 0))],
        out_specs=pl.BlockSpec((tile, 2 * cols), lambda i: (i, 0)),
        out_shape=jax.ShapeDtypeStruct((rows, 2 * cols), data.dtype),
        cost_estimate=pl.CostEstimate(flops=0, bytes_accessed=6 * rows * cols, transcendentals=0),
        name="keep",
    )(labels, data)


def place_kernel(pieces, parts, labels, *refs):
    got, out, sems = refs[: len(pieces)], refs[-2], refs[-1]
    tile = out.shape[0] // parts
    blocks = out.shape[1] // BLOCK // 2
    half = my_half()
    leaves = [(labels[b] == half).astype(jnp.int32) for b in range(blocks)]
    copies = []
    for ref, first in zip(got, pieces):
        for block, at, size, before in runs(first, ref.shape[0] // tile, parts):
            copy = pltpu.make_async_copy(
                ref.at[pl.ds(before * tile, size * tile), :],
                out.at[pl.ds(at * tile, size * tile), lanes(blocks + nth(leaves, block))],
                sems.at[len(copies)],
            )
            copies.append((block < sum(leaves), copy))
    for valid, copy in copies:
        pl.when(valid)(copy.start)
    for valid, copy in copies:
        pl.when(valid)(copy.wait)


def place(labels, got, held, pieces, parts):
    tile = held.shape[0] // parts
    count = sum(len(runs(first, x.shape[0] // tile, parts)) for x, first in zip(got, pieces))
    moved = sum(x.size for x in got)
    return pl.pallas_call(
        functools.partial(place_kernel, pieces, parts),
        in_specs=[pl.BlockSpec(memory_space=pltpu.SMEM)]
        + [pl.BlockSpec(memory_space=pltpu.VMEM)] * len(got)
        + [pl.BlockSpec(memory_space=pl.ANY)],
        out_specs=pl.BlockSpec(memory_space=pl.ANY),
        out_shape=jax.ShapeDtypeStruct(held.shape, held.dtype),
        input_output_aliases={len(got) + 1: 0},
        scratch_shapes=[pltpu.SemaphoreType.DMA((count,))],
        cost_estimate=pl.CostEstimate(flops=0, bytes_accessed=4 * moved, transcendentals=0),
    )(labels, *got, held)


def with_gram(part, factor):
    gram = jnp.dot(factor, factor.T, preferred_element_type=jnp.float32)
    return jnp.concatenate([part, jnp.pad(gram, ((0, 0), (0, BLOCK - factor.shape[0])))], axis=1)


def steps(data, labels, w_init, h_init):
    rows, cols = data.shape
    blocks = cols // BLOCK
    groups = lax.axis_size("cell")
    across = groups // 2
    odd = lax.axis_index("cell") & 1
    most = blocks - max(1, blocks // 4)
    parts = next(p for p in (8, 4, 2) if rows % (16 * p) == 0)
    labels = labels[:, 0]
    always = max(1, most - 1) * parts
    rest = most * parts - always
    cuts = [always * share // 16 for share in SHARES]
    packed = [pack(labels, data, cuts[i], cuts[i + 1] - cuts[i], parts) for i in range(len(cuts) - 1)]
    own_0 = pack(labels, data, always, rest // 2, parts)
    own_1 = pack(labels, data, always + rest // 2, rest - rest // 2, parts)

    def send(i):
        return flipped(packed[i], "cell", across)

    got = [send(0)]
    lent = flipped(own_1, "cell", 1)
    labels_in = flipped(labels, "cell", across)
    half = my_half()
    leaving = jnp.maximum(jnp.sum((labels != half).astype(jnp.int32)), jnp.sum((labels_in == half).astype(jnp.int32)))
    need = (leaving * parts > always).astype(jnp.int32)
    need_beside = flipped(need[None], "cell", 1)[0]
    w_factor = w_init
    h_factor = h_init
    children = keep(labels, data)
    for step in range(ITERS):
        w_round = w_factor.astype(jnp.bfloat16)
        w_part = jnp.dot(w_round, data, preferred_element_type=jnp.float32)
        w_sum = all_sum(with_gram(w_part, w_round), "gene")
        h_factor = update_rows(h_factor, w_sum[:, :cols], w_sum[:, cols : cols + 2])
        h_round = h_factor.astype(jnp.bfloat16)
        h_part = lax.dot_general(
            h_round, data, (((1,), (1,)), ((), ())), preferred_element_type=jnp.float32
        )
        h_sum = all_sum(with_gram(h_part, h_round), "cell")
        got.append(send(step + 1))
        w_factor = update_rows(w_factor, h_sum[:, :rows], h_sum[:, rows : rows + 2])
    for i in range(len(got) - 1):
        children = place(labels_in, [got[i]], children, [cuts[i]], parts)

    def late(parity):
        def exchange(own, beside):
            return (
                lax.ppermute(own, "cell", [(i, i ^ across) for i in range(groups) if i % 2 == parity]),
                lax.ppermute(beside, "cell", [(i ^ 1, i ^ across) for i in range(groups) if i % 2 == parity]),
            )

        return exchange

    def late_both(own, beside):
        return flipped(own, "cell", across), flipped(beside, "cell", across | 1)

    wanted = (need << odd) + (need_beside << (1 - odd))
    last = lax.switch(wanted, [lambda *x: x, late(0), late(1), late_both], own_0, lent)
    children = place(
        labels_in, [got[-1], *last], children, [cuts[-2], always, always + rest // 2], parts
    )
    return (w_factor, h_factor, children)


SHARES = (0, 5, 12, 16)


def solution(mesh):
    placed = (P("gene", "cell"), P("cell", None), P(None, "gene"), P(None, "cell"))
    return jax.shard_map(
        steps,
        mesh=mesh,
        in_specs=placed,
        out_specs=(P(None, "gene"), P(None, "cell"), P("gene", "cell")),
        check_vma=False,
    )
```

time: 211 us -> 213 us (level)
  the two profiles are of different devices: /device:TPU:28 before, /device:TPU:0 now
where the time goes in v2:
time: 213 us; the launch traced here: 210 us
  waiting for transfers between devices  112 us (53%)
  Pallas kernels  27.7 us (13%)
  starting transfers between devices  25.2 us (12%)
  other arithmetic  18.1 us (8%)
  matrix products  15.6 us (7%)
  between operations  7.8 us (4%)
  local copies, waits for them, and re-layouts  3.43 us (2%)
    ppermute x20, waiting for transfers between devices, flipped(): return lax.ppermute(x, axis, [(i, i ^ mask) for i in range(count)])  112 us
    ppermute x20, starting transfers between devices, flipped(): return lax.ppermute(x, axis, [(i, i ^ mask) for i in range(count)])  25.2 us
    pallas_call x5, Pallas kernels, pack(): pl.pallas_call(functools.partial(pack_kernel, first, parts), in_specs=[pl...  12.8 us
    pallas_call x1, Pallas kernels, keep(): pl.pallas_call(functools.partial(keep_kernel, cols // BLOCK), grid=(rows...  8.52 us
    dot_general x2, matrix products, steps(): lax.dot_general(h_round, data, (((1,), (1,)), ((), ())), preferred_elemen...  7.78 us
    dot_general x2, matrix products, steps(): w_part = jnp.dot(w_round, data, preferred_element_type=jnp.float32)  6.46 us
    pallas_call x3, Pallas kernels, place(): pl.pallas_call(functools.partial(place_kernel, pieces, parts), in_specs=[...  6.31 us
    another operation x4, other arithmetic  5.88 us
  transfers between devices with their start and end apart: 20, of which 9 were waited for; matrix products, arithmetic and copies ran while one was open for 8% of the time, Pallas kernels for 12%

profile of v2, /device:TPU:0, one launch (start us, length us, event | category | flops | bytes accessed | tf_op | source)
XLA Modules:
  0.0 209.8 jit_solution(15611965201068845546)
XLA Ops:
  0.6 1.0 fusion.8
  1.6 3.3 %fusion.10 = f32[2,512]{1,0:T(2,128)S(1)} fusion(bf16[4992,512]{1,0:T(8,128)(2,1)} %data.11, f32[2,4992]{1,0:T(2,128)} %param.10), kind=kOutput, calls=%fused_computation.25 | convolution fusion | flops 10233600 | bytes 5155840 | tf_op jit(solution)/shard_map/dot_general | solution.py:204
  5.4 2.5 %collective-permute-start.7 = (f32[2,640]{1,0:T(2,128)S(1)}, f32[2,640]{1,0:T(2,128)S(1)}, u32[]{:S(2)}, u32[]{:S(2)}) collective-permute-start(f32[2,640]{1,0:T(2,128)S(1)} %select_maximum_fusion.3), channel_id=1, source_target_pairs={{0,16},{8,24},{16,0},{24,8},{1,17},{9,25},{17,1},{25,9},{2,18},{10... | collective-permute-start | bytes 15368 | tf_op jit(solution)/shard_map/ppermute | solution.py:19
  8.0 1.5 collective-permute-done.7
  9.5 1.4 collective-permute-done.8
  12.9 1.3 fusion.32
  14.2 1.3 fusion.34
  15.5 3.9 %fusion.40 = f32[2,4992]{1,0:T(2,128)S(1)} fusion(bf16[2,512]{1,0:T(2,128)(2,1)S(1)} %pad_maximum_fusion.3, bf16[4992,512]{1,0:T(8,128)(2,1)} %data.11), kind=kOutput, calls=%fused_computation.66 | convolution fusion | flops 10223616 | bytes 5153792 | tf_op jit(solution)/shard_map/dot_general | solution.py:208
  19.6 2.7 %collective-permute-start.10 = (f32[2,5120]{1,0:T(2,128)S(1)}, f32[2,5120]{1,0:T(2,128)S(1)}, u32[]{:S(2)}, u32[]{:S(2)}) collective-permute-start(f32[2,5120]{1,0:T(2,128)S(1)} %select_maximum_fusion.1), channel_id=1, source_target_pairs={{0,4},{1,5},{2,6},{3,7},{4,0},{5,1},{6,2},{7,3},{8,12},{9,13},{10,... | collective-permute-start | bytes 122888 | tf_op jit(solution)/shard_map/ppermute | solution.py:19
  22.2 1.3 collective-permute-start.11
  23.8 1.2 collective-permute-done.10
  25.0 3.0 %collective-permute-done.11 = f32[2,5120]{1,0:T(2,128)S(1)} collective-permute-done((f32[2,5120]{1,0:T(2,128)S(1)}, f32[2,5120]{1,0:T(2,128)S(1)}, u32[]{:S(2)}, u32[]{:S(2)}) %collective-permute-start.11) | collective-permute-done | bytes 40992 | tf_op jit(solution)/shard_map/ppermute | solution.py:19
  28.1 1.6 collective-permute-start.12
  29.6 2.5 %collective-permute-done.12 = f32[2,5120]{1,0:T(2,128)S(1)} collective-permute-done((f32[2,5120]{1,0:T(2,128)S(1)}, f32[2,5120]{1,0:T(2,128)S(1)}, u32[]{:S(2)}, u32[]{:S(2)}) %collective-permute-start.12) | collective-permute-done | bytes 40992 | tf_op jit(solution)/shard_map/ppermute | solution.py:19
  34.0 1.3 fusion.28
  35.4 2.0 fusion.30
  37.4 3.2 %fusion.42 = f32[2,512]{1,0:T(2,128)S(1)} fusion(bf16[2,4992]{1,0:T(2,128)(2,1)S(1)} %pad_maximum_fusion.1, bf16[4992,512]{1,0:T(8,128)(2,1)} %data.11), kind=kOutput, calls=%fused_computation.68 | convolution fusion | flops 10223616 | bytes 5135872 | tf_op jit(solution)/shard_map/dot_general | solution.py:204
  40.8 0.7 collective-permute-start.14
  41.4 1.2 collective-permute-start.15
  42.6 1.4 collective-permute-start.20
  44.0 2.6 %shard_map.69 = bf16[2496,128]{1,0:T(8,128)(2,1)} custom-call(s32[4]{0:T(128)} %bitcast.16.labels, bf16[4992,512]{1,0:T(8,128)(2,1)} %data.11), custom_call_target="tpu_custom_call" | custom-call | bytes 1277952 | tf_op jit(solution)/shard_map/pallas_call | solution.py:98
  46.7 1.6 collective-permute-start.23
  50.1 2.5 %fusion.19 = (f32[1,512]{1,0:T(1,128)S(1)}, f32[1,512]{1,0:T(1,128)S(1)}) fusion(f32[1,512]{1,0:T(1,128)S(1)} %get-tuple-element.40, f32[2,640]{1,0:T(2,128)S(1)} %add_add_fusion.2, f32[]{:T(128)S(6)} %add.141, f32[]{:T(128)} %bitcast.11, f32[]{:T(128)} %bitcast.10, f32[1,512]{1,0:T(1,128)S(1)} %get-tuple-element.38, f32[]{:T(128)S(6)} %add.139, f32[]{:T(128)} %bitcast.9, ...), kind=kLoop, calls=%fused_computation.51 | loop fusion | flops 7168 | bytes 12312 | tf_op jit(solution)/shard_map/max | solution.py:45
  52.6 3.9 %fusion.22 = f32[2,4992]{1,0:T(2,128)S(1)} fusion(bf16[4992,512]{1,0:T(8,128)(2,1)} %data.11, f32[2,512]{1,0:T(2,128)S(1)} %pad_maximum_fusion.2), kind=kOutput, calls=%fused_computation.54 | convolution fusion | flops 10224640 | bytes 5155840 | tf_op jit(solution)/shard_map/dot_general | solution.py:208
  57.3 1.5 collective-permute-start.16
  58.9 2.8 %collective-permute-start.18 = (f32[2,5120]{1,0:T(2,128)}, f32[2,5120]{1,0:T(2,128)}, u32[]{:S(2)}, u32[]{:S(2)}) collective-permute-start(f32[2,5120]{1,0:T(2,128)} %select_maximum_fusion), channel_id=1, source_target_pairs={{0,6},{1,7},{2,4},{3,5},{4,2},{5,3},{6,0},{7,1},{8,14},{9,15},{10,... | collective-permute-start | bytes 122888 | tf_op jit(solution)/shard_map/ppermute | solution.py:19
  61.7 1.3 fusion.24
  63.0 1.8 shard_map.68
  64.8 8.5 %keep.1.refs_1_ = bf16[4992,1024]{1,0:T(8,128)(2,1)} custom-call(s32[4]{0:T(128)} %bitcast.16.labels, bf16[4992,512]{1,0:T(8,128)(2,1)} %data.11), custom_call_target="tpu_custom_call" | custom-call | bytes 15335424 | tf_op jit(solution)/shard_map/keep/pallas_call | solution.py:119
  73.3 2.7 %shard_map.71 = bf16[3120,128]{1,0:T(8,128)(2,1)} custom-call(s32[4]{0:T(128)} %bitcast.16.labels, bf16[4992,512]{1,0:T(8,128)(2,1)} %data.11), custom_call_target="tpu_custom_call" | custom-call | bytes 1597440 | tf_op jit(solution)/shard_map/pallas_call | solution.py:98
  76.0 2.9 %shard_map.70 = bf16[4368,128]{1,0:T(8,128)(2,1)} custom-call(s32[4]{0:T(128)} %bitcast.16.labels, bf16[4992,512]{1,0:T(8,128)(2,1)} %data.11), custom_call_target="tpu_custom_call" | custom-call | bytes 2236416 | tf_op jit(solution)/shard_map/pallas_call | solution.py:98
  79.0 2.8 %shard_map.67 = bf16[2496,128]{1,0:T(8,128)(2,1)} custom-call(s32[4]{0:T(128)} %bitcast.16.labels, bf16[4992,512]{1,0:T(8,128)(2,1)} %data.11), custom_call_target="tpu_custom_call" | custom-call | bytes 1277952 | tf_op jit(solution)/shard_map/pallas_call | solution.py:98
  81.8 0.7 collective-permute-start.25
  82.5 2.3 %collective-permute-start.24 = (bf16[4368,128]{1,0:T(8,128)(2,1)S(1)}, bf16[4368,128]{1,0:T(8,128)(2,1)S(1)}, u32[]{:S(2)}, u32[]{:S(2)}) collective-permute-start(bf16[4368,128]{1,0:T(8,128)(2,1)S(1)} %copy-done.1), channel_id=1, source_target_pairs={{0,4},{1,5},{2,6},{3,7},{4,0},{5,1},{6,2},{7,3},{8,12},{9,13},{10,... | collective-permute-start | bytes 3354632 | tf_op jit(solution)/shard_map/ppermute | solution.py:19
  84.9 1.5 add_add_fusion
  86.9 1.3 fusion.25
  89.4 2.9 %collective-permute-start.22 = (s32[1]{0:T(128)}, s32[1]{0:T(128)}, u32[]{:S(2)}, u32[]{:S(2)}) collective-permute-start(s32[1]{0:T(128)} %bitcast.17), channel_id=1, source_target_pairs={{0,1},{1,0},{2,3},{3,2},{4,5},{5,4},{6,7},{7,6},{8,9},{9,8},{10,11... | collective-permute-start | bytes 20 | tf_op jit(solution)/shard_map/ppermute | solution.py:19
  92.3 0.7 collective-permute-done.22
  93.0 0.7 collective-permute-start.21
  94.3 0.8 add.146
  97.0 3.2 %fusion.7 = (f32[1,4992]{1,0:T(1,128)S(1)}, f32[1,4992]{1,0:T(1,128)S(1)}) fusion(f32[1,4992]{1,0:T(1,128)} %get-tuple-element.36, f32[2,5120]{1,0:T(2,128)S(1)} %add.146, f32[]{:T(128)S(6)} %add.149, f32[]{:T(128)} %bitcast.15, f32[]{:T(128)} %bitcast.14, f32[1,4992]{1,0:T(1,128)} %copy-done.3, f32[]{:T(128)S(6)} %add.147, f32[]{:T(128)} %bitcast.13, ...), kind=kLoop, calls=%fused_computation.22 | loop fusion | flops 69888 | bytes 119832 | tf_op jit(solution)/shard_map/max | solution.py:45
  100.9 69.3 %collective-permute-done.25.refs_0_ = bf16[3120,128]{1,0:T(8,128)(2,1)} collective-permute-done((bf16[3120,128]{1,0:T(8,128)(2,1)}, bf16[3120,128]{1,0:T(8,128)(2,1)}, u32[]{:S(2)}, u32[]{:S(2)}) %collective-permute-start.25) | collective-permute-done | bytes 798752 | tf_op jit(solution)/shard_map/ppermute | solution.py:19
  170.3 2.1 shard_map.72.refs_1_
  172.4 21.8 %collective-permute-done.24.refs_0_ = bf16[4368,128]{1,0:T(8,128)(2,1)S(1)} collective-permute-done((bf16[4368,128]{1,0:T(8,128)(2,1)S(1)}, bf16[4368,128]{1,0:T(8,128)(2,1)S(1)}, u32[]{:S(2)}, u32[]{:S(2)}) %collective-permute-start.24) | collective-permute-done | bytes 1118240 | tf_op jit(solution)/shard_map/ppermute | solution.py:19
  194.2 1.0 copy-done
  195.2 2.3 %shard_map.73.refs_3_ = bf16[4992,1024]{1,0:T(8,128)(2,1)} custom-call(s32[4]{0:T(128)} %collective-permute-done.20.labels, bf16[4368,128]{1,0:T(8,128)(2,1)} %copy-done, bf16[4992,1024]{1,0:T(8,128)(2,1)} %shard_map.72.refs_1_), custom_call_target="tpu_custom_call", output_to_operand_aliasing={{}: (2, {})} | custom-call | bytes 2236416 | tf_op jit(solution)/shard_map/pallas_call | solution.py:155
  197.5 10.4 %collective-permute-done.21.refs_0_ = bf16[2496,128]{1,0:T(8,128)(2,1)} collective-permute-done((bf16[2496,128]{1,0:T(8,128)(2,1)}, bf16[2496,128]{1,0:T(8,128)(2,1)}, u32[]{:S(2)}, u32[]{:S(2)}) %collective-permute-start.21) | collective-permute-done | bytes 639008 | tf_op jit(solution)/shard_map/ppermute | solution.py:19
  207.9 2.0 shard_map.74
  (52 shorter events, 5.8 us)
Async XLA Ops:
  0.6 12.2 %copy-start.6 = (f32[2,512]{1,0:T(2,128)S(1)}, f32[2,512]{1,0:T(2,128)}, u32[]{:S(2)}) copy-start(f32[2,512]{1,0:T(2,128)} %param.11) | copy-start | bytes 12292
  1.6 32.4 %copy-start.2 = (f32[2,4992]{1,0:T(2,128)S(1)}, f32[2,4992]{1,0:T(2,128)}, u32[]{:S(2)}) copy-start(f32[2,4992]{1,0:T(2,128)} %param.10) | copy-start | bytes 119812
  4.9 3.1 %collective-permute-start.6 = (f32[2,640]{1,0:T(2,128)S(1)}, f32[2,640]{1,0:T(2,128)S(1)}, u32[]{:S(2)}, u32[]{:S(2)}) collective-permute-start(f32[2,640]{1,0:T(2,128)S(1)} %select_maximum_fusion.3), channel_id=1, source_target_pairs={{0,8},{8,0},{16,24},{24,16},{1,9},{9,1},{17,25},{25,17},{2,10},{10... | collective-permute-start | bytes 15368 | tf_op jit(solution)/shard_map/ppermute | solution.py:19
  5.4 4.1 %collective-permute-start.7 = (f32[2,640]{1,0:T(2,128)S(1)}, f32[2,640]{1,0:T(2,128)S(1)}, u32[]{:S(2)}, u32[]{:S(2)}) collective-permute-start(f32[2,640]{1,0:T(2,128)S(1)} %select_maximum_fusion.3), channel_id=1, source_target_pairs={{0,16},{8,24},{16,0},{24,8},{1,17},{9,25},{17,1},{25,9},{2,18},{10... | collective-permute-start | bytes 15368 | tf_op jit(solution)/shard_map/ppermute | solution.py:19
  8.0 3.0 %collective-permute-start.8 = (f32[2,640]{1,0:T(2,128)S(1)}, f32[2,640]{1,0:T(2,128)S(1)}, u32[]{:S(2)}, u32[]{:S(2)}) collective-permute-start(f32[2,640]{1,0:T(2,128)S(1)} %select_maximum_fusion.3), channel_id=1, source_target_pairs={{0,24},{8,16},{16,8},{24,0},{1,25},{9,17},{17,9},{25,1},{2,26},{10... | collective-permute-start | bytes 15368 | tf_op jit(solution)/shard_map/ppermute | solution.py:19
  19.6 5.4 %collective-permute-start.10 = (f32[2,5120]{1,0:T(2,128)S(1)}, f32[2,5120]{1,0:T(2,128)S(1)}, u32[]{:S(2)}, u32[]{:S(2)}) collective-permute-start(f32[2,5120]{1,0:T(2,128)S(1)} %select_maximum_fusion.1), channel_id=1, source_target_pairs={{0,4},{1,5},{2,6},{3,7},{4,0},{5,1},{6,2},{7,3},{8,12},{9,13},{10,... | collective-permute-start | bytes 122888 | tf_op jit(solution)/shard_map/ppermute | solution.py:19
  22.2 5.8 %collective-permute-start.11 = (f32[2,5120]{1,0:T(2,128)S(1)}, f32[2,5120]{1,0:T(2,128)S(1)}, u32[]{:S(2)}, u32[]{:S(2)}) collective-permute-start(f32[2,5120]{1,0:T(2,128)S(1)} %select_maximum_fusion.1), channel_id=1, source_target_pairs={{0,6},{1,7},{2,4},{3,5},{4,2},{5,3},{6,0},{7,1},{8,14},{9,15},{10,... | collective-permute-start | bytes 122888 | tf_op jit(solution)/shard_map/ppermute | solution.py:19
  23.6 4.5 %collective-permute-start.9 = (f32[2,5120]{1,0:T(2,128)S(1)}, f32[2,5120]{1,0:T(2,128)S(1)}, u32[]{:S(2)}, u32[]{:S(2)}) collective-permute-start(f32[2,5120]{1,0:T(2,128)S(1)} %select_maximum_fusion.1), channel_id=1, source_target_pairs={{0,2},{1,3},{2,0},{3,1},{4,6},{5,7},{6,4},{7,5},{8,10},{9,11},{10,... | collective-permute-start | bytes 122888 | tf_op jit(solution)/shard_map/ppermute | solution.py:19
  28.1 4.1 %collective-permute-start.12 = (f32[2,5120]{1,0:T(2,128)S(1)}, f32[2,5120]{1,0:T(2,128)S(1)}, u32[]{:S(2)}, u32[]{:S(2)}) collective-permute-start(f32[2,5120]{1,0:T(2,128)S(1)} %add_add_fusion.1), channel_id=1, source_target_pairs={{0,1},{1,0},{2,3},{3,2},{4,5},{5,4},{6,7},{7,6},{8,9},{9,8},{10,11... | collective-permute-start | bytes 122888 | tf_op jit(solution)/shard_map/ppermute | solution.py:19
  35.4 8.7 %copy-start.3 = (f32[1,4992]{1,0:T(1,128)}, f32[1,4992]{1,0:T(1,128)S(1)}, u32[]{:S(2)}) copy-start(f32[1,4992]{1,0:T(1,128)S(1)} %get-tuple-element.34) | copy-start | bytes 59908
  40.8 7.5 %collective-permute-start.13 = (f32[2,640]{1,0:T(2,128)S(1)}, f32[2,640]{1,0:T(2,128)S(1)}, u32[]{:S(2)}, u32[]{:S(2)}) collective-permute-start(f32[2,640]{1,0:T(2,128)S(1)} %select_maximum_fusion.2), channel_id=1, source_target_pairs={{0,8},{8,0},{16,24},{24,16},{1,9},{9,1},{17,25},{25,17},{2,10},{10... | collective-permute-start | bytes 15368 | tf_op jit(solution)/shard_map/ppermute | solution.py:19
  40.8 7.5 %collective-permute-start.14 = (f32[2,640]{1,0:T(2,128)S(1)}, f32[2,640]{1,0:T(2,128)S(1)}, u32[]{:S(2)}, u32[]{:S(2)}) collective-permute-start(f32[2,640]{1,0:T(2,128)S(1)} %select_maximum_fusion.2), channel_id=1, source_target_pairs={{0,16},{8,24},{16,0},{24,8},{1,17},{9,25},{17,1},{25,9},{2,18},{10... | collective-permute-start | bytes 15368 | tf_op jit(solution)/shard_map/ppermute | solution.py:19
  41.4 6.8 %collective-permute-start.15 = (f32[2,640]{1,0:T(2,128)S(1)}, f32[2,640]{1,0:T(2,128)S(1)}, u32[]{:S(2)}, u32[]{:S(2)}) collective-permute-start(f32[2,640]{1,0:T(2,128)S(1)} %select_maximum_fusion.2), channel_id=1, source_target_pairs={{0,24},{8,16},{16,8},{24,0},{1,25},{9,17},{17,9},{25,1},{2,26},{10... | collective-permute-start | bytes 15368 | tf_op jit(solution)/shard_map/ppermute | solution.py:19
  42.6 44.2 %collective-permute-start.20 = (s32[4]{0:T(128)}, s32[4]{0:T(128)}, u32[]{:S(2)}, u32[]{:S(2)}) collective-permute-start(s32[4]{0:T(128)} %bitcast.16.labels), channel_id=1, source_target_pairs={{0,4},{1,5},{2,6},{3,7},{4,0},{5,1},{6,2},{7,3},{8,12},{9,13},{10,... | collective-permute-start | bytes 56 | tf_op jit(solution)/shard_map/ppermute | solution.py:19
  46.7 54.3 %collective-permute-start.23 = (bf16[2496,128]{1,0:T(8,128)(2,1)}, bf16[2496,128]{1,0:T(8,128)(2,1)S(1)}, u32[]{:S(2)}, u32[]{:S(2)}) collective-permute-start(bf16[2496,128]{1,0:T(8,128)(2,1)} %shard_map.69), channel_id=1, source_target_pairs={{0,1},{1,0},{2,3},{3,2},{4,5},{5,4},{6,7},{7,6},{8,9},{9,8},{10,11... | collective-permute-start | bytes 1916936 | tf_op jit(solution)/shard_map/ppermute | solution.py:19
  52.6 9.1 %copy-start.5 = (f32[2,512]{1,0:T(2,128)}, f32[2,512]{1,0:T(2,128)S(1)}, u32[]{:S(2)}) copy-start(f32[2,512]{1,0:T(2,128)S(1)} %pad_maximum_fusion.2) | copy-start | bytes 12292
  56.7 5.0 %copy-start.7 = (f32[2,2]{1,0:T(2,128)}, f32[2,2]{1,0:T(2,128)S(1)}, u32[]{:S(2)}) copy-start(f32[2,2]{1,0:T(2,128)S(1)} %fusion.20) | copy-start | bytes 52
  57.3 24.5 %collective-permute-start.16 = (f32[2,5120]{1,0:T(2,128)}, f32[2,5120]{1,0:T(2,128)S(1)}, u32[]{:S(2)}, u32[]{:S(2)}) collective-permute-start(f32[2,5120]{1,0:T(2,128)} %select_maximum_fusion), channel_id=1, source_target_pairs={{0,2},{1,3},{2,0},{3,1},{4,6},{5,7},{6,4},{7,5},{8,10},{9,11},{10,... | collective-permute-start | bytes 122888 | tf_op jit(solution)/shard_map/ppermute | solution.py:19
  58.8 23.8 %collective-permute-start.17 = (f32[2,5120]{1,0:T(2,128)}, f32[2,5120]{1,0:T(2,128)}, u32[]{:S(2)}, u32[]{:S(2)}) collective-permute-start(f32[2,5120]{1,0:T(2,128)} %select_maximum_fusion), channel_id=1, source_target_pairs={{0,4},{1,5},{2,6},{3,7},{4,0},{5,1},{6,2},{7,3},{8,12},{9,13},{10,... | collective-permute-start | bytes 122888 | tf_op jit(solution)/shard_map/ppermute | solution.py:19
  58.9 26.0 %collective-permute-start.18 = (f32[2,5120]{1,0:T(2,128)}, f32[2,5120]{1,0:T(2,128)}, u32[]{:S(2)}, u32[]{:S(2)}) collective-permute-start(f32[2,5120]{1,0:T(2,128)} %select_maximum_fusion), channel_id=1, source_target_pairs={{0,6},{1,7},{2,4},{3,5},{4,2},{5,3},{6,0},{7,1},{8,14},{9,15},{10,... | collective-permute-start | bytes 122888 | tf_op jit(solution)/shard_map/ppermute | solution.py:19
  79.0 3.6 %copy-start.1 = (bf16[4368,128]{1,0:T(8,128)(2,1)S(1)}, bf16[4368,128]{1,0:T(8,128)(2,1)}, u32[]{:S(2)}) copy-start(bf16[4368,128]{1,0:T(8,128)(2,1)} %shard_map.70) | copy-start | bytes 3354628
  81.8 0.7 copy-start.4
  81.8 88.5 %collective-permute-start.25 = (bf16[3120,128]{1,0:T(8,128)(2,1)}, bf16[3120,128]{1,0:T(8,128)(2,1)}, u32[]{:S(2)}, u32[]{:S(2)}) collective-permute-start(bf16[3120,128]{1,0:T(8,128)(2,1)} %shard_map.71), channel_id=1, source_target_pairs={{0,4},{1,5},{2,6},{3,7},{4,0},{5,1},{6,2},{7,3},{8,12},{9,13},{10,... | collective-permute-start | bytes 2396168 | tf_op jit(solution)/shard_map/ppermute | solution.py:19
  82.5 111.6 %collective-permute-start.24 = (bf16[4368,128]{1,0:T(8,128)(2,1)S(1)}, bf16[4368,128]{1,0:T(8,128)(2,1)S(1)}, u32[]{:S(2)}, u32[]{:S(2)}) collective-permute-start(bf16[4368,128]{1,0:T(8,128)(2,1)S(1)} %copy-done.1), channel_id=1, source_target_pairs={{0,4},{1,5},{2,6},{3,7},{4,0},{5,1},{6,2},{7,3},{8,12},{9,13},{10,... | collective-permute-start | bytes 3354632 | tf_op jit(solution)/shard_map/ppermute | solution.py:19
  86.4 8.0 %collective-permute-start.19 = (f32[2,5120]{1,0:T(2,128)}, f32[2,5120]{1,0:T(2,128)}, u32[]{:S(2)}, u32[]{:S(2)}) collective-permute-start(f32[2,5120]{1,0:T(2,128)} %add_add_fusion), channel_id=1, source_target_pairs={{0,1},{1,0},{2,3},{3,2},{4,5},{5,4},{6,7},{7,6},{8,9},{9,8},{10,11... | collective-permute-start | bytes 122888 | tf_op jit(solution)/shard_map/ppermute | solution.py:19
  89.4 3.6 %collective-permute-start.22 = (s32[1]{0:T(128)}, s32[1]{0:T(128)}, u32[]{:S(2)}, u32[]{:S(2)}) collective-permute-start(s32[1]{0:T(128)} %bitcast.17), channel_id=1, source_target_pairs={{0,1},{1,0},{2,3},{3,2},{4,5},{5,4},{6,7},{7,6},{8,9},{9,8},{10,11... | collective-permute-start | bytes 20 | tf_op jit(solution)/shard_map/ppermute | solution.py:19
  93.0 114.8 %collective-permute-start.21 = (bf16[2496,128]{1,0:T(8,128)(2,1)}, bf16[2496,128]{1,0:T(8,128)(2,1)}, u32[]{:S(2)}, u32[]{:S(2)}) collective-permute-start(bf16[2496,128]{1,0:T(8,128)(2,1)} %shard_map.67), channel_id=1, source_target_pairs={{0,4},{1,5},{2,6},{3,7},{4,0},{5,1},{6,2},{7,3},{8,12},{9,13},{10,... | collective-permute-start | bytes 1916936 | tf_op jit(solution)/shard_map/ppermute | solution.py:19
  194.2 1.0 copy-start

commit v3 on v2

--- a/solution.py
+++ b/solution.py
@@ -19,21 +19,36 @@
     return lax.ppermute(x, axis, [(i, i ^ mask) for i in range(count)])
 
 
-def all_sum(x, axis):
-    count = lax.axis_size(axis)
-    if count & (count - 1):
-        return lax.psum(x, axis)
-    bit = count
+def all_sum(x, axis, bit):
     while bit > 1:
         high, low = bit >> 1, bit >> 2
         if low:
             x = (x + flipped(x, axis, low)) + (flipped(x, axis, high) + flipped(x, axis, high | low))
         else:
             x = x + flipped(x, axis, high)
-        bit = low or high
-        if not low:
-            break
+        bit = low
     return x
+
+
+def row_sum(x, axis):
+    odd = lax.axis_index(axis) & 1
+    mine = jnp.where(odd > 0, x[1:], x[:1]) + flipped(jnp.where(odd > 0, x[:1], x[1:]), axis, 1)
+    count, bit = lax.axis_size(axis), 2
+    while bit < count:
+        both = bit << 1 < count
+        if both:
+            high = bit << 1
+            mine = (mine + flipped(mine, axis, bit)) + (flipped(mine, axis, high) + flipped(mine, axis, high | bit))
+        else:
+            mine = mine + flipped(mine, axis, bit)
+        bit = bit << (2 if both else 1)
+    return mine
+
+
+def join_rows(mine, axis):
+    odd = lax.axis_index(axis) & 1
+    other = flipped(mine, axis, 1)
+    return jnp.concatenate([jnp.where(odd > 0, other, mine), jnp.where(odd > 0, mine, other)])
 
 
 def update_rows(factor, numer, gram):
@@ -99,7 +114,7 @@
         functools.partial(pack_kernel, first, parts),
         in_specs=[pl.BlockSpec(memory_space=pltpu.SMEM), pl.BlockSpec(memory_space=pl.ANY)],
         out_specs=pl.BlockSpec(memory_space=pltpu.VMEM),
-        out_shape=jax.ShapeDtypeStruct(shape, data.dtype),
+        out_shape=pltpu.VMEM(shape, data.dtype),
         scratch_shapes=[pltpu.SemaphoreType.DMA((len(runs(first, count, parts)),))],
         cost_estimate=pl.CostEstimate(flops=0, bytes_accessed=4 * shape[0] * BLOCK, transcendentals=0),
     )(labels, data)
@@ -182,7 +197,9 @@
     always = max(1, most - 1) * parts
     rest = most * parts - always
     cuts = [always * share // 16 for share in SHARES]
-    packed = [pack(labels, data, cuts[i], cuts[i + 1] - cuts[i], parts) for i in range(len(cuts) - 1)]
+    packed = []
+    for i in range(len(cuts) - 1):
+        packed.append(pack(labels, data, cuts[i], cuts[i + 1] - cuts[i], parts))
     own_0 = pack(labels, data, always, rest // 2, parts)
     own_1 = pack(labels, data, always + rest // 2, rest - rest // 2, parts)
 
@@ -202,39 +219,48 @@
     for step in range(ITERS):
         w_round = w_factor.astype(jnp.bfloat16)
         w_part = jnp.dot(w_round, data, preferred_element_type=jnp.float32)
-        w_sum = all_sum(with_gram(w_part, w_round), "gene")
+        w_sum = all_sum(with_gram(w_part, w_round), "gene", lax.axis_size("gene"))
         h_factor = update_rows(h_factor, w_sum[:, :cols], w_sum[:, cols : cols + 2])
         h_round = h_factor.astype(jnp.bfloat16)
         h_part = lax.dot_general(
             h_round, data, (((1,), (1,)), ((), ())), preferred_element_type=jnp.float32
         )
-        h_sum = all_sum(with_gram(h_part, h_round), "cell")
+        h_row = row_sum(with_gram(h_part, h_round), "cell")
         got.append(send(step + 1))
-        w_factor = update_rows(w_factor, h_sum[:, :rows], h_sum[:, rows : rows + 2])
-    for i in range(len(got) - 1):
-        children = place(labels_in, [got[i]], children, [cuts[i]], parts)
-
-    def late(parity):
-        def exchange(own, beside):
+
+        def finish(w_factor, h_row):
+            h_sum = join_rows(h_row, "cell")
+            return update_rows(w_factor, h_sum[:, :rows], h_sum[:, rows : rows + 2])
+
+        if step + 1 < ITERS:
+            w_factor = finish(w_factor, h_row)
+    children = place(labels_in, got[:-1], children, cuts[:-2], parts)
+
+    def late_none(own, beside, w_factor, h_row):
+        return jnp.zeros_like(own), jnp.zeros_like(beside), finish(w_factor, h_row)
+
+    def late_one(parity):
+        def exchange(own, beside, w_factor, h_row):
             return (
                 lax.ppermute(own, "cell", [(i, i ^ across) for i in range(groups) if i % 2 == parity]),
                 lax.ppermute(beside, "cell", [(i ^ 1, i ^ across) for i in range(groups) if i % 2 == parity]),
+                finish(w_factor, h_row),
             )
 
         return exchange
 
-    def late_both(own, beside):
-        return flipped(own, "cell", across), flipped(beside, "cell", across | 1)
+    def late_both(own, beside, w_factor, h_row):
+        return flipped(own, "cell", across), flipped(beside, "cell", across | 1), finish(w_factor, h_row)
 
     wanted = (need << odd) + (need_beside << (1 - odd))
-    last = lax.switch(wanted, [lambda *x: x, late(0), late(1), late_both], own_0, lent)
+    *last, w_factor = lax.switch(wanted, [late_none, late_one(0), late_one(1), late_both], own_0, lent, w_factor, h_row)
     children = place(
         labels_in, [got[-1], *last], children, [cuts[-2], always, always + rest // 2], parts
     )
     return (w_factor, h_factor, children)
 
 
-SHARES = (0, 5, 12, 16)
+SHARES = (0, 4, 13, 16)
 
 
 def solution(mesh):

time: 213 us -> 189 us (0.89)
  the two profiles are of different devices: /device:TPU:0 before, /device:TPU:12 now
where the time goes in v3:
time: 189 us; the launch traced here: 188 us
  waiting for transfers between devices  93 us (49%)
  starting transfers between devices  29.6 us (16%)
  Pallas kernels  24 us (13%)
  matrix products  15.6 us (8%)
  other arithmetic  14.7 us (8%)
  between operations  6.53 us (3%)
  local copies, waits for them, and re-layouts  3.44 us (2%)
    ppermute x22, waiting for transfers between devices, flipped(): return lax.ppermute(x, axis, [(i, i ^ mask) for i in range(count)])  67.5 us
    ppermute x22, starting transfers between devices, flipped(): return lax.ppermute(x, axis, [(i, i ^ mask) for i in range(count)])  25.5 us
    ppermute x1, waiting for transfers between devices, exchange(): lax.ppermute(own, 'cell', [(i, i ^ across) for i in range(groups) if i %...  25.5 us
    pallas_call x5, Pallas kernels, pack(): pl.pallas_call(functools.partial(pack_kernel, first, parts), in_specs=[pl...  9.92 us
    pallas_call x1, Pallas kernels, keep(): pl.pallas_call(functools.partial(keep_kernel, cols // BLOCK), grid=(rows...  8.5 us
    dot_general x2, matrix products, steps(): lax.dot_general(h_round, data, (((1,), (1,)), ((), ())), preferred_elemen...  7.79 us
    max x3, other arithmetic, update_rows(): jnp.maximum(factor[1] + (numer[1] - gram[1, 0] * first - gram[1, 1] * fac...  7.6 us
    dot_general x2, matrix products, steps(): w_part = jnp.dot(w_round, data, preferred_element_type=jnp.float32)  6.47 us
  transfers between devices with their start and end apart: 24, of which 11 were waited for; matrix products, arithmetic and copies ran while one was open for 11% of the time, Pallas kernels for 11%

profile of v3, /device:TPU:12, one launch (start us, length us, event | category | flops | bytes accessed | tf_op | source)
XLA Modules:
  0.0 188.3 jit_solution(16732751220457889512)
XLA Ops:
  0.6 1.0 fusion.3
  1.6 3.3 %fusion.5 = f32[2,512]{1,0:T(2,128)S(1)} fusion(bf16[4992,512]{1,0:T(8,128)(2,1)} %data.11, f32[2,4992]{1,0:T(2,128)} %param.10), kind=kOutput, calls=%fused_computation.53 | convolution fusion | flops 10233600 | bytes 5155840 | tf_op jit(solution)/shard_map/dot_general | solution.py:221
  4.9 1.6 collective-permute-start.13
  6.8 1.8 collective-permute-done.13
  8.6 0.9 collective-permute-done.14
  11.4 1.2 fusion.24
  12.6 1.3 fusion.26
  13.9 3.9 %fusion.40 = f32[2,4992]{1,0:T(2,128)S(1)} fusion(bf16[2,512]{1,0:T(2,128)(2,1)S(1)} %pad_maximum_fusion.6, bf16[4992,512]{1,0:T(8,128)(2,1)} %data.11), kind=kOutput, calls=%fused_computation.102 | convolution fusion | flops 10223616 | bytes 5153792 | tf_op jit(solution)/shard_map/dot_general | solution.py:225
  18.6 3.3 %collective-permute-done.15 = f32[1,5120]{1,0:T(1,128)S(1)} collective-permute-done((f32[1,5120]{1,0:T(1,128)S(1)}, f32[1,5120]{1,0:T(1,128)S(1)}, u32[]{:S(2)}, u32[]{:S(2)}) %collective-permute-start.15) | collective-permute-done | bytes 20512 | tf_op jit(solution)/shard_map/ppermute | solution.py:19
  22.4 2.6 %collective-permute-start.17 = (f32[1,5120]{1,0:T(1,128)S(1)}, f32[1,5120]{1,0:T(1,128)S(1)}, u32[]{:S(2)}, u32[]{:S(2)}) collective-permute-start(f32[1,5120]{1,0:T(1,128)S(1)} %fusion), channel_id=1, source_target_pairs={{0,4},{1,5},{2,6},{3,7},{4,0},{5,1},{6,2},{7,3},{8,12},{9,13},{10,... | collective-permute-start | bytes 61448 | tf_op jit(solution)/shard_map/ppermute | solution.py:19
  25.8 1.4 collective-permute-done.17
  27.1 1.7 collective-permute-done.18
  29.4 2.1 %collective-permute-start.10 = (s32[4]{0:T(128)S(1)}, s32[4]{0:T(128)S(1)}, u32[]{:S(2)}, u32[]{:S(2)}) collective-permute-start(s32[4]{0:T(128)S(1)} %bitcast.48), channel_id=1, source_target_pairs={{0,4},{1,5},{2,6},{3,7},{4,0},{5,1},{6,2},{7,3},{8,12},{9,13},{10,... | collective-permute-start | bytes 56 | tf_op jit(solution)/shard_map/ppermute | solution.py:19
  31.6 2.6 %shard_map.68 = bf16[2496,128]{1,0:T(8,128)(2,1)} custom-call(s32[4]{0:T(128)} %bitcast.42, bf16[4992,512]{1,0:T(8,128)(2,1)} %data.11), custom_call_target="tpu_custom_call" | custom-call | bytes 1277952 | tf_op jit(solution)/shard_map/pallas_call | solution.py:113
  34.2 1.6 collective-permute-start.27
  37.7 1.4 slice_reduce_fusion.11
  39.1 1.4 slice_reduce_fusion.8
  40.5 3.2 %fusion.42 = f32[2,512]{1,0:T(2,128)S(1)} fusion(bf16[2,4992]{1,0:T(2,128)(2,1)S(1)} %pad_maximum_fusion.4, bf16[4992,512]{1,0:T(8,128)(2,1)} %data.11), kind=kOutput, calls=%fused_computation.104 | convolution fusion | flops 10223616 | bytes 5135872 | tf_op jit(solution)/shard_map/dot_general | solution.py:221
  43.9 0.7 collective-permute-start.21
  44.6 1.2 collective-permute-start.22
  45.8 0.6 fusion.19
  46.4 1.8 shard_map.67
  48.2 2.1 %shard_map.71 = bf16[5616,128]{1,0:T(8,128)(2,1)S(1)} custom-call(s32[4]{0:T(128)} %bitcast.44, bf16[4992,512]{1,0:T(8,128)(2,1)} %data.11), custom_call_target="tpu_custom_call" | custom-call | bytes 2875392 | tf_op jit(solution)/shard_map/pallas_call | solution.py:113
  50.3 1.8 shard_map.70
  52.0 1.7 shard_map.69
  53.8 0.9 collective-permute-start.30
  56.6 2.5 %fusion.14 = (f32[1,512]{1,0:T(1,128)S(1)}, f32[1,512]{1,0:T(1,128)S(1)}) fusion(f32[1,512]{1,0:T(1,128)S(1)} %get-tuple-element.82, f32[2,640]{1,0:T(2,128)S(1)} %add_add_fusion.2, f32[]{:T(128)S(6)} %add.175, f32[]{:T(128)} %bitcast.30, f32[]{:T(128)} %bitcast.29, f32[1,512]{1,0:T(1,128)S(1)} %get-tuple-element.80, f32[]{:T(128)S(6)} %add.173, ...), kind=kLoop, calls=%fused_computation.79 | loop fusion | flops 7168 | bytes 12312 | tf_op jit(solution)/shard_map/max | solution.py:60
  59.1 3.9 %fusion.17 = f32[2,4992]{1,0:T(2,128)S(1)} fusion(bf16[4992,512]{1,0:T(8,128)(2,1)} %data.11, f32[2,512]{1,0:T(2,128)S(1)} %pad_maximum_fusion.5), kind=kOutput, calls=%fused_computation.83 | convolution fusion | flops 10224640 | bytes 5155840 | tf_op jit(solution)/shard_map/dot_general | solution.py:225
  63.8 0.6 fusion.20
  65.7 2.9 %collective-permute-start.11 = (s32[1]{0:T(128)}, s32[1]{0:T(128)}, u32[]{:S(2)}, u32[]{:S(2)}) collective-permute-start(s32[1]{0:T(128)} %bitcast.17), channel_id=1, source_target_pairs={{0,1},{1,0},{2,3},{3,2},{4,5},{5,4},{6,7},{7,6},{8,9},{9,8},{10,11... | collective-permute-start | bytes 20 | tf_op jit(solution)/shard_map/ppermute | solution.py:19
  68.5 0.9 collective-permute-done.11
  70.0 3.4 %collective-permute-start.24 = (f32[1,5120]{1,0:T(1,128)S(1)}, f32[1,5120]{1,0:T(1,128)S(1)}, u32[]{:S(2)}, u32[]{:S(2)}) collective-permute-start(f32[1,5120]{1,0:T(1,128)S(1)} %fusion.1), channel_id=1, source_target_pairs={{0,2},{1,3},{2,0},{3,1},{4,6},{5,7},{6,4},{7,5},{8,10},{9,11},{10,... | collective-permute-start | bytes 61448 | tf_op jit(solution)/shard_map/ppermute | solution.py:19
  73.6 1.4 collective-permute-start.26
  75.0 2.5 %add_maximum_fusion.8 = (f32[4992]{0:T(1024)S(1)}, f32[4992]{0:T(1024)S(1)}) fusion(f32[4992]{0:T(1024)S(1)} %get-tuple-element.63, f32[4992]{0:T(1024)S(1)} %get-tuple-element.128, f32[]{:T(128)S(6)} %add.168, f32[]{:T(128)} %bitcast.26, f32[]{:T(128)} %bitcast.25, f32[4992]{0:T(1024)S(1)} %get-tuple-element.64, f32[]{:T(128)S(6)} %add.166, f32[]{:T(128)} %bitcast.24, ...), kind=kLoop, calls=%fused_computation.39 | loop fusion | flops 69888 | bytes 119832 | tf_op jit(solution)/shard_map/max | solution.py:60
  77.5 13.1 %collective-permute-done.24 = f32[1,5120]{1,0:T(1,128)S(1)} collective-permute-done((f32[1,5120]{1,0:T(1,128)S(1)}, f32[1,5120]{1,0:T(1,128)S(1)}, u32[]{:S(2)}, u32[]{:S(2)}) %collective-permute-start.24) | collective-permute-done | bytes 20512 | tf_op jit(solution)/shard_map/ppermute | solution.py:19
  90.7 41.7 %collective-permute-done.25 = f32[1,5120]{1,0:T(1,128)S(1)} collective-permute-done((f32[1,5120]{1,0:T(1,128)S(1)}, f32[1,5120]{1,0:T(1,128)S(1)}, u32[]{:S(2)}, u32[]{:S(2)}) %collective-permute-start.25) | collective-permute-done | bytes 20512 | tf_op jit(solution)/shard_map/ppermute | solution.py:19
  132.4 2.4 %collective-permute-done.26 = f32[1,5120]{1,0:T(1,128)S(1)} collective-permute-done((f32[1,5120]{1,0:T(1,128)S(1)}, f32[1,5120]{1,0:T(1,128)S(1)}, u32[]{:S(2)}, u32[]{:S(2)}) %collective-permute-start.26) | collective-permute-done | bytes 20512 | tf_op jit(solution)/shard_map/ppermute | solution.py:19
  134.9 35.0 %conditional.1 = (bf16[2496,128]{1,0:T(8,128)(2,1)}, bf16[2496,128]{1,0:T(8,128)(2,1)}, f32[2,4992]{1,0:T(2,128)S(1)}) conditional(s32[]{:T(128)} %clamp.3, (f32[1,5120]{1,0:T(1,128)S(1)}, f32[4992]{0:T(1024)S(1)}, f32[4992]{0:T(1024)S(1)}) %tuple.24, (bf16[2496,128]{1,0:T(8,128)(2,1)S(1)}, ...), branch_computations={%region_2.3_spmd, %region_3.4_spmd, %region_4.5_spmd, %region_5.6_... | conditional | flops 90118 | bytes 5635338 | solution.py:256
  135.5 2.8 %collective-permute-start.4 = (bf16[2496,128]{1,0:T(8,128)(2,1)S(1)}, bf16[2496,128]{1,0:T(8,128)(2,1)}, u32[]{:S(2)}, u32[]{:S(2)}) collective-permute-start(bf16[2496,128]{1,0:T(8,128)(2,1)S(1)} %get-tuple-element.44), channel_id=1, source_target_pairs={{1,5},{3,7},{5,1},{7,3},{9,13},{11,15},{13,9},{15,11},{17,21},{19,... | collective-permute-start | bytes 1916936 | tf_op jit(solution)/shard_map/cond/branch_2_fun/ppermute | solution.py:245
  138.3 1.3 collective-permute-start.5
  139.6 0.7 fusion.32
  141.7 2.6 %add_maximum_fusion.4 = (f32[4992]{0:T(1024)S(1)}, f32[4992]{0:T(1024)S(1)}) fusion(f32[4992]{0:T(1024)S(1)} %get-tuple-element.48, f32[4992]{0:T(1024)S(1)} %get-tuple-element.109, f32[]{:T(128)S(6)} %add.111, f32[]{:T(128)} %bitcast.11, f32[]{:T(128)} %bitcast.10, f32[4992]{0:T(1024)S(1)} %get-tuple-element.46, f32[]{:T(128)S(6)} %add.109, f32[]{:T(128)} %bitcast.9, ...), kind=kLoop, calls=%fused_computation.17 | loop fusion | flops 69888 | bytes 119832 | tf_op jit(solution)/shard_map/cond/branch_2_fun/max | solution.py:60
  144.3 25.5 %collective-permute-done.4 = bf16[2496,128]{1,0:T(8,128)(2,1)} collective-permute-done((bf16[2496,128]{1,0:T(8,128)(2,1)S(1)}, bf16[2496,128]{1,0:T(8,128)(2,1)}, u32[]{:S(2)}, u32[]{:S(2)}) %collective-permute-start.4) | collective-permute-done | bytes 639008 | tf_op jit(solution)/shard_map/cond/branch_2_fun/ppermute | solution.py:245
  169.8 3.5 %collective-permute-start.28 = (bf16[1872,128]{1,0:T(8,128)(2,1)S(1)}, bf16[1872,128]{1,0:T(8,128)(2,1)S(1)}, u32[]{:S(2)}, u32[]{:S(2)}) collective-permute-start(bf16[1872,128]{1,0:T(8,128)(2,1)S(1)} %shard_map.69), channel_id=1, source_target_pairs={{0,4},{1,5},{2,6},{3,7},{4,0},{5,1},{6,2},{7,3},{8,12},{9,13},{10,... | collective-permute-start | bytes 1437704 | tf_op jit(solution)/shard_map/ppermute | solution.py:19
  173.3 8.5 %keep.1.refs_2_ = bf16[4992,1024]{1,0:T(8,128)(2,1)} custom-call(s32[4]{0:T(128)} %bitcast.47, bf16[4992,512]{1,0:T(8,128)(2,1)} %data.11), custom_call_target="tpu_custom_call" | custom-call | bytes 15335424 | tf_op jit(solution)/shard_map/keep/pallas_call | solution.py:134
  181.9 2.9 %shard_map.72.refs_3_ = bf16[4992,1024]{1,0:T(8,128)(2,1)} custom-call(s32[4]{0:T(128)} %copy-done.7, bf16[2496,128]{1,0:T(8,128)(2,1)} %collective-permute-done.29.refs_0_, bf16[5616,128]{1,0:T(8,128)(2,1)} %collective-permute-done.30.refs_1_, bf16[4992,1024]{1,0:T(8,128)(2,1)} %keep.1.refs_2_), custom_call_target="tpu_custom_call", output_to_operand_aliasing={{}: (3, {})} | custom-call | bytes 4153344 | tf_op jit(solution)/shard_map/pallas_call | solution.py:170
  184.8 0.8 copy-done
  185.6 2.7 %shard_map.73 = bf16[4992,1024]{1,0:T(8,128)(2,1)} custom-call(s32[4]{0:T(128)} %copy-done.7, bf16[1872,128]{1,0:T(8,128)(2,1)} %copy-done, bf16[2496,128]{1,0:T(8,128)(2,1)} %get-tuple-element.61.refs_1_, bf16[2496,128]{1,0:T(8,128)(2,1)} %get-tuple-element.62.refs_2_, bf16[4992,1024]{1,0:T(8,128)(2,1)} %shard_map.72.refs_3_), custom_call_target="tpu_custom_call", output_to_operand_aliasing={{}: (4, {})} | custom-call | bytes 3514368 | tf_op jit(solution)/shard_map/pallas_call | solution.py:170
  (67 shorter events, 6.9 us)
Async XLA Ops:
  0.6 10.7 %copy-start.6 = (f32[2,512]{1,0:T(2,128)S(1)}, f32[2,512]{1,0:T(2,128)}, u32[]{:S(2)}) copy-start(f32[2,512]{1,0:T(2,128)} %param.11) | copy-start | bytes 12292
  1.6 27.8 %copy-start.3 = (s32[4,1]{0,1:T(1,128)S(1)}, s32[4,1]{0,1:T(1,128)}, u32[]{:S(2)}) copy-start(s32[4,1]{0,1:T(1,128)} %param.9) | copy-start | bytes 52
  4.9 1.9 collective-permute-start.12
  4.9 3.7 %collective-permute-start.13 = (f32[2,640]{1,0:T(2,128)S(1)}, f32[2,640]{1,0:T(2,128)S(1)}, u32[]{:S(2)}, u32[]{:S(2)}) collective-permute-start(f32[2,640]{1,0:T(2,128)S(1)} %select_maximum_fusion.3), channel_id=1, source_target_pairs={{0,16},{8,24},{16,0},{24,8},{1,17},{9,25},{17,1},{25,9},{2,18},{10... | collective-permute-start | bytes 15368 | tf_op jit(solution)/shard_map/ppermute | solution.py:19
  6.5 3.0 %collective-permute-start.14 = (f32[2,640]{1,0:T(2,128)S(1)}, f32[2,640]{1,0:T(2,128)S(1)}, u32[]{:S(2)}, u32[]{:S(2)}) collective-permute-start(f32[2,640]{1,0:T(2,128)S(1)} %select_maximum_fusion.3), channel_id=1, source_target_pairs={{0,24},{8,16},{16,8},{24,0},{1,25},{9,17},{17,9},{25,1},{2,26},{10... | collective-permute-start | bytes 15368 | tf_op jit(solution)/shard_map/ppermute | solution.py:19
  13.9 23.7 %copy-start.1 = (f32[2,4992]{1,0:T(2,128)S(1)}, f32[2,4992]{1,0:T(2,128)}, u32[]{:S(2)}) copy-start(f32[2,4992]{1,0:T(2,128)} %param.10) | copy-start | bytes 119812
  18.0 3.8 %collective-permute-start.15 = (f32[1,5120]{1,0:T(1,128)S(1)}, f32[1,5120]{1,0:T(1,128)S(1)}, u32[]{:S(2)}, u32[]{:S(2)}) collective-permute-start(f32[1,5120]{1,0:T(1,128)S(1)} %broadcast_select_fusion.12), channel_id=1, source_target_pairs={{0,1},{1,0},{2,3},{3,2},{4,5},{5,4},{6,7},{7,6},{8,9},{9,8},{10,11... | collective-permute-start | bytes 61448 | tf_op jit(solution)/shard_map/ppermute | solution.py:19
  21.9 3.8 %collective-permute-start.16 = (f32[1,5120]{1,0:T(1,128)S(1)}, f32[1,5120]{1,0:T(1,128)S(1)}, u32[]{:S(2)}, u32[]{:S(2)}) collective-permute-start(f32[1,5120]{1,0:T(1,128)S(1)} %fusion), channel_id=1, source_target_pairs={{0,2},{1,3},{2,0},{3,1},{4,6},{5,7},{6,4},{7,5},{8,10},{9,11},{10,... | collective-permute-start | bytes 61448 | tf_op jit(solution)/shard_map/ppermute | solution.py:19
  22.4 4.7 %collective-permute-start.17 = (f32[1,5120]{1,0:T(1,128)S(1)}, f32[1,5120]{1,0:T(1,128)S(1)}, u32[]{:S(2)}, u32[]{:S(2)}) collective-permute-start(f32[1,5120]{1,0:T(1,128)S(1)} %fusion), channel_id=1, source_target_pairs={{0,4},{1,5},{2,6},{3,7},{4,0},{5,1},{6,2},{7,3},{8,12},{9,13},{10,... | collective-permute-start | bytes 61448 | tf_op jit(solution)/shard_map/ppermute | solution.py:19
  25.0 3.8 %collective-permute-start.18 = (f32[1,5120]{1,0:T(1,128)S(1)}, f32[1,5120]{1,0:T(1,128)S(1)}, u32[]{:S(2)}, u32[]{:S(2)}) collective-permute-start(f32[1,5120]{1,0:T(1,128)S(1)} %fusion), channel_id=1, source_target_pairs={{0,6},{1,7},{2,4},{3,5},{4,2},{5,3},{6,0},{7,1},{8,14},{9,15},{10,... | collective-permute-start | bytes 61448 | tf_op jit(solution)/shard_map/ppermute | solution.py:19
  28.9 6.9 %collective-permute-start.19 = (f32[1,5120]{1,0:T(1,128)S(1)}, f32[1,5120]{1,0:T(1,128)S(1)}, u32[]{:S(2)}, u32[]{:S(2)}) collective-permute-start(f32[1,5120]{1,0:T(1,128)S(1)} %add_add_fusion.1), channel_id=1, source_target_pairs={{0,1},{1,0},{2,3},{3,2},{4,5},{5,4},{6,7},{7,6},{8,9},{9,8},{10,11... | collective-permute-start | bytes 61448 | tf_op jit(solution)/shard_map/ppermute | solution.py:19
  29.4 16.4 %copy-start.4 = (s32[4,1]{0,1:T(1,128)S(1)}, s32[4,1]{0,1:T(1,128)}, u32[]{:S(2)}) copy-start(s32[4,1]{0,1:T(1,128)} %param.9) | copy-start | bytes 52
  29.4 34.4 %collective-permute-start.10 = (s32[4]{0:T(128)S(1)}, s32[4]{0:T(128)S(1)}, u32[]{:S(2)}, u32[]{:S(2)}) collective-permute-start(s32[4]{0:T(128)S(1)} %bitcast.48), channel_id=1, source_target_pairs={{0,4},{1,5},{2,6},{3,7},{4,0},{5,1},{6,2},{7,3},{8,12},{9,13},{10,... | collective-permute-start | bytes 56 | tf_op jit(solution)/shard_map/ppermute | solution.py:19
  34.2 100.7 %collective-permute-start.27 = (bf16[2496,128]{1,0:T(8,128)(2,1)}, bf16[2496,128]{1,0:T(8,128)(2,1)}, u32[]{:S(2)}, u32[]{:S(2)}) collective-permute-start(bf16[2496,128]{1,0:T(8,128)(2,1)} %shard_map.68), channel_id=1, source_target_pairs={{0,1},{1,0},{2,3},{3,2},{4,5},{5,4},{6,7},{7,6},{8,9},{9,8},{10,11... | collective-permute-start | bytes 1916936 | tf_op jit(solution)/shard_map/ppermute | solution.py:19
  43.9 9.9 %collective-permute-start.20 = (f32[2,640]{1,0:T(2,128)S(1)}, f32[2,640]{1,0:T(2,128)S(1)}, u32[]{:S(2)}, u32[]{:S(2)}) collective-permute-start(f32[2,640]{1,0:T(2,128)S(1)} %select_maximum_fusion.2), channel_id=1, source_target_pairs={{0,8},{8,0},{16,24},{24,16},{1,9},{9,1},{17,25},{25,17},{2,10},{10... | collective-permute-start | bytes 15368 | tf_op jit(solution)/shard_map/ppermute | solution.py:19
  43.9 10.7 %collective-permute-start.21 = (f32[2,640]{1,0:T(2,128)S(1)}, f32[2,640]{1,0:T(2,128)S(1)}, u32[]{:S(2)}, u32[]{:S(2)}) collective-permute-start(f32[2,640]{1,0:T(2,128)S(1)} %select_maximum_fusion.2), channel_id=1, source_target_pairs={{0,16},{8,24},{16,0},{24,8},{1,17},{9,25},{17,1},{25,9},{2,18},{10... | collective-permute-start | bytes 15368 | tf_op jit(solution)/shard_map/ppermute | solution.py:19
  44.6 10.1 %collective-permute-start.22 = (f32[2,640]{1,0:T(2,128)S(1)}, f32[2,640]{1,0:T(2,128)S(1)}, u32[]{:S(2)}, u32[]{:S(2)}) collective-permute-start(f32[2,640]{1,0:T(2,128)S(1)} %select_maximum_fusion.2), channel_id=1, source_target_pairs={{0,24},{8,16},{16,8},{24,0},{1,25},{9,17},{17,9},{25,1},{2,26},{10... | collective-permute-start | bytes 15368 | tf_op jit(solution)/shard_map/ppermute | solution.py:19
  53.8 128.1 %collective-permute-start.30 = (bf16[5616,128]{1,0:T(8,128)(2,1)S(1)}, bf16[5616,128]{1,0:T(8,128)(2,1)}, u32[]{:S(2)}, u32[]{:S(2)}) collective-permute-start(bf16[5616,128]{1,0:T(8,128)(2,1)S(1)} %shard_map.71), channel_id=1, source_target_pairs={{0,4},{1,5},{2,6},{3,7},{4,0},{5,1},{6,2},{7,3},{8,12},{9,13},{10,... | collective-permute-start | bytes 4313096 | tf_op jit(solution)/shard_map/ppermute | solution.py:19
  59.1 122.7 %copy-start.5 = (f32[2,512]{1,0:T(2,128)}, f32[2,512]{1,0:T(2,128)S(1)}, u32[]{:S(2)}) copy-start(f32[2,512]{1,0:T(2,128)S(1)} %pad_maximum_fusion.5) | copy-start | bytes 12292
  63.2 6.7 %collective-permute-start.23 = (f32[1,5120]{1,0:T(1,128)S(1)}, f32[1,5120]{1,0:T(1,128)S(1)}, u32[]{:S(2)}, u32[]{:S(2)}) collective-permute-start(f32[1,5120]{1,0:T(1,128)S(1)} %broadcast_select_fusion.8), channel_id=1, source_target_pairs={{0,1},{1,0},{2,3},{3,2},{4,5},{5,4},{6,7},{7,6},{8,9},{9,8},{10,11... | collective-permute-start | bytes 61448 | tf_op jit(solution)/shard_map/ppermute | solution.py:19
  63.8 118.0 %copy-start.7 = (s32[4]{0:T(128)}, s32[4]{0:T(128)S(1)}, u32[]{:S(2)}) copy-start(s32[4]{0:T(128)S(1)} %collective-permute-done.10.labels) | copy-start | bytes 52
  65.7 3.7 %collective-permute-start.11 = (s32[1]{0:T(128)}, s32[1]{0:T(128)}, u32[]{:S(2)}, u32[]{:S(2)}) collective-permute-start(s32[1]{0:T(128)} %bitcast.17), channel_id=1, source_target_pairs={{0,1},{1,0},{2,3},{3,2},{4,5},{5,4},{6,7},{7,6},{8,9},{9,8},{10,11... | collective-permute-start | bytes 20 | tf_op jit(solution)/shard_map/ppermute | solution.py:19
  70.0 20.6 %collective-permute-start.24 = (f32[1,5120]{1,0:T(1,128)S(1)}, f32[1,5120]{1,0:T(1,128)S(1)}, u32[]{:S(2)}, u32[]{:S(2)}) collective-permute-start(f32[1,5120]{1,0:T(1,128)S(1)} %fusion.1), channel_id=1, source_target_pairs={{0,2},{1,3},{2,0},{3,1},{4,6},{5,7},{6,4},{7,5},{8,10},{9,11},{10,... | collective-permute-start | bytes 61448 | tf_op jit(solution)/shard_map/ppermute | solution.py:19
  73.5 58.9 %collective-permute-start.25 = (f32[1,5120]{1,0:T(1,128)S(1)}, f32[1,5120]{1,0:T(1,128)S(1)}, u32[]{:S(2)}, u32[]{:S(2)}) collective-permute-start(f32[1,5120]{1,0:T(1,128)S(1)} %fusion.1), channel_id=1, source_target_pairs={{0,4},{1,5},{2,6},{3,7},{4,0},{5,1},{6,2},{7,3},{8,12},{9,13},{10,... | collective-permute-start | bytes 61448 | tf_op jit(solution)/shard_map/ppermute | solution.py:19
  73.6 61.2 %collective-permute-start.26 = (f32[1,5120]{1,0:T(1,128)S(1)}, f32[1,5120]{1,0:T(1,128)S(1)}, u32[]{:S(2)}, u32[]{:S(2)}) collective-permute-start(f32[1,5120]{1,0:T(1,128)S(1)} %fusion.1), channel_id=1, source_target_pairs={{0,6},{1,7},{2,4},{3,5},{4,2},{5,3},{6,0},{7,1},{8,14},{9,15},{10,... | collective-permute-start | bytes 61448 | tf_op jit(solution)/shard_map/ppermute | solution.py:19
  90.7 91.2 %collective-permute-start.29 = (bf16[2496,128]{1,0:T(8,128)(2,1)S(1)}, bf16[2496,128]{1,0:T(8,128)(2,1)}, u32[]{:S(2)}, u32[]{:S(2)}) collective-permute-start(bf16[2496,128]{1,0:T(8,128)(2,1)S(1)} %shard_map.70), channel_id=1, source_target_pairs={{0,4},{1,5},{2,6},{3,7},{4,0},{5,1},{6,2},{7,3},{8,12},{9,13},{10,... | collective-permute-start | bytes 1916936 | tf_op jit(solution)/shard_map/ppermute | solution.py:19
  134.9 4.7 %collective-permute-start.6 = (f32[1,5120]{1,0:T(1,128)S(1)}, f32[1,5120]{1,0:T(1,128)S(1)}, u32[]{:S(2)}, u32[]{:S(2)}) collective-permute-start(f32[1,5120]{1,0:T(1,128)S(1)} %get-tuple-element.47), channel_id=1, source_target_pairs={{0,1},{1,0},{2,3},{3,2},{4,5},{5,4},{6,7},{7,6},{8,9},{9,8},{10,11... | collective-permute-start | bytes 61448 | tf_op jit(solution)/shard_map/cond/branch_2_fun/ppermute | solution.py:19
  135.5 34.4 %collective-permute-start.4 = (bf16[2496,128]{1,0:T(8,128)(2,1)S(1)}, bf16[2496,128]{1,0:T(8,128)(2,1)}, u32[]{:S(2)}, u32[]{:S(2)}) collective-permute-start(bf16[2496,128]{1,0:T(8,128)(2,1)S(1)} %get-tuple-element.44), channel_id=1, source_target_pairs={{1,5},{3,7},{5,1},{7,3},{9,13},{11,15},{13,9},{15,11},{17,21},{19,... | collective-permute-start | bytes 1916936 | tf_op jit(solution)/shard_map/cond/branch_2_fun/ppermute | solution.py:245
  138.3 31.5 %collective-permute-start.5 = (bf16[2496,128]{1,0:T(8,128)(2,1)}, bf16[2496,128]{1,0:T(8,128)(2,1)}, u32[]{:S(2)}, u32[]{:S(2)}) collective-permute-start(bf16[2496,128]{1,0:T(8,128)(2,1)} %get-tuple-element.45), channel_id=1, source_target_pairs={{0,5},{2,7},{4,1},{6,3},{8,13},{10,15},{12,9},{14,11},{16,21},{18,... | collective-permute-start | bytes 1916936 | tf_op jit(solution)/shard_map/cond/branch_2_fun/ppermute | solution.py:246
  169.8 12.0 %copy-start.2 = (f32[2,4992]{1,0:T(2,128)}, f32[2,4992]{1,0:T(2,128)S(1)}, u32[]{:S(2)}) copy-start(f32[2,4992]{1,0:T(2,128)S(1)} %get-tuple-element.57) | copy-start | bytes 119812
  169.8 15.0 %collective-permute-start.28 = (bf16[1872,128]{1,0:T(8,128)(2,1)S(1)}, bf16[1872,128]{1,0:T(8,128)(2,1)S(1)}, u32[]{:S(2)}, u32[]{:S(2)}) collective-permute-start(bf16[1872,128]{1,0:T(8,128)(2,1)S(1)} %shard_map.69), channel_id=1, source_target_pairs={{0,4},{1,5},{2,6},{3,7},{4,0},{5,1},{6,2},{7,3},{8,12},{9,13},{10,... | collective-permute-start | bytes 1437704 | tf_op jit(solution)/shard_map/ppermute | solution.py:19
  184.8 0.8 copy-start

commit v4 on v3

--- a/solution.py
+++ b/solution.py
@@ -192,11 +192,11 @@
     across = groups // 2
     odd = lax.axis_index("cell") & 1
     most = blocks - max(1, blocks // 4)
-    parts = next(p for p in (8, 4, 2) if rows % (16 * p) == 0)
+    parts = next(p for p in (39, 8, 4, 2) if rows % (16 * p) == 0)
     labels = labels[:, 0]
     always = max(1, most - 1) * parts
     rest = most * parts - always
-    cuts = [always * share // 16 for share in SHARES]
+    cuts = [always * share // 78 for share in SHARES]
     packed = []
     for i in range(len(cuts) - 1):
         packed.append(pack(labels, data, cuts[i], cuts[i + 1] - cuts[i], parts))
@@ -260,7 +260,7 @@
     return (w_factor, h_factor, children)
 
 
-SHARES = (0, 4, 13, 16)
+SHARES = (0, 21, 59, 78)
 
 
 def solution(mesh):

time: 189 us -> 189 us (level)
    ppermute x22, waiting for transfers between devices: 67.5 us -> 62.5 us  [flipped(): return lax.ppermute(x, axis, [(i, i ^ mask) for i in range(count)])]
    ppermute x1, waiting for transfers between devices: 25.5 us -> 29.3 us  [exchange(): lax.ppermute(own, 'cell', [(i, i ^ across) for i in range(groups) if i %...]
  transfers between devices with their start and end apart: 24 -> 24, of which waited for: 11 -> 12; matrix products, arithmetic and copies ran while one was open for 11% -> 11% of each run, Pallas kernels for 11% -> 11%
where the time goes in v4:
time: 189 us; the launch traced here: 188 us
  waiting for transfers between devices  91.8 us (49%)
  starting transfers between devices  30.2 us (16%)
  Pallas kernels  23.2 us (12%)
  matrix products  15.6 us (8%)
  other arithmetic  14.8 us (8%)
  between operations  6.61 us (3%)
  local copies, waits for them, and re-layouts  4.3 us (2%)
    ppermute x22, waiting for transfers between devices, flipped(): return lax.ppermute(x, axis, [(i, i ^ mask) for i in range(count)])  62.5 us
    ppermute x1, waiting for transfers between devices, exchange(): lax.ppermute(own, 'cell', [(i, i ^ across) for i in range(groups) if i %...  29.3 us
    ppermute x22, starting transfers between devices, flipped(): return lax.ppermute(x, axis, [(i, i ^ mask) for i in range(count)])  26 us
    pallas_call x5, Pallas kernels, pack(): pl.pallas_call(functools.partial(pack_kernel, first, parts), in_specs=[pl...  9.09 us
    pallas_call x1, Pallas kernels, keep(): pl.pallas_call(functools.partial(keep_kernel, cols // BLOCK), grid=(rows...  8.5 us
    dot_general x2, matrix products, steps(): lax.dot_general(h_round, data, (((1,), (1,)), ((), ())), preferred_elemen...  7.79 us
    max x3, other arithmetic, update_rows(): jnp.maximum(factor[1] + (numer[1] - gram[1, 0] * first - gram[1, 1] * fac...  7.61 us
    dot_general x2, matrix products, steps(): w_part = jnp.dot(w_round, data, preferred_element_type=jnp.float32)  6.47 us
  transfers between devices with their start and end apart: 24, of which 12 were waited for; matrix products, arithmetic and copies ran while one was open for 11% of the time, Pallas kernels for 11%

profile of v4, /device:TPU:12, one launch (start us, length us, event | category | flops | bytes accessed | tf_op | source)
XLA Modules:
  0.0 187.8 jit_solution(12379279498893471243)
XLA Ops:
  0.6 1.0 fusion.3
  1.6 3.3 %fusion.5 = f32[2,512]{1,0:T(2,128)S(1)} fusion(bf16[4992,512]{1,0:T(8,128)(2,1)} %data.11, f32[2,4992]{1,0:T(2,128)} %param.10), kind=kOutput, calls=%fused_computation.53 | convolution fusion | flops 10233600 | bytes 5155840 | tf_op jit(solution)/shard_map/dot_general | solution.py:221
  4.9 1.6 collective-permute-start.13
  6.8 1.8 collective-permute-done.13
  8.6 0.9 collective-permute-done.14
  11.4 1.3 fusion.24
  12.7 1.3 fusion.26
  14.1 3.9 %fusion.40 = f32[2,4992]{1,0:T(2,128)S(1)} fusion(bf16[2,512]{1,0:T(2,128)(2,1)S(1)} %pad_maximum_fusion.6, bf16[4992,512]{1,0:T(8,128)(2,1)} %data.11), kind=kOutput, calls=%fused_computation.102 | convolution fusion | flops 10223616 | bytes 5153792 | tf_op jit(solution)/shard_map/dot_general | solution.py:225
  18.7 3.3 %collective-permute-done.15 = f32[1,5120]{1,0:T(1,128)S(1)} collective-permute-done((f32[1,5120]{1,0:T(1,128)S(1)}, f32[1,5120]{1,0:T(1,128)S(1)}, u32[]{:S(2)}, u32[]{:S(2)}) %collective-permute-start.15) | collective-permute-done | bytes 20512 | tf_op jit(solution)/shard_map/ppermute | solution.py:19
  22.6 2.6 %collective-permute-start.17 = (f32[1,5120]{1,0:T(1,128)S(1)}, f32[1,5120]{1,0:T(1,128)S(1)}, u32[]{:S(2)}, u32[]{:S(2)}) collective-permute-start(f32[1,5120]{1,0:T(1,128)S(1)} %fusion), channel_id=1, source_target_pairs={{0,4},{1,5},{2,6},{3,7},{4,0},{5,1},{6,2},{7,3},{8,12},{9,13},{10,... | collective-permute-start | bytes 61448 | tf_op jit(solution)/shard_map/ppermute | solution.py:19
  25.9 1.4 collective-permute-done.17
  27.3 1.7 collective-permute-done.18
  29.6 2.1 %collective-permute-start.10 = (s32[4]{0:T(128)S(1)}, s32[4]{0:T(128)S(1)}, u32[]{:S(2)}, u32[]{:S(2)}) collective-permute-start(s32[4]{0:T(128)S(1)} %bitcast.48), channel_id=1, source_target_pairs={{0,4},{1,5},{2,6},{3,7},{4,0},{5,1},{6,2},{7,3},{8,12},{9,13},{10,... | collective-permute-start | bytes 56 | tf_op jit(solution)/shard_map/ppermute | solution.py:19
  31.7 1.8 shard_map.68
  33.5 1.6 collective-permute-start.27
  36.9 1.4 slice_reduce_fusion.11
  38.4 1.3 slice_reduce_fusion.8
  39.7 3.2 %fusion.42 = f32[2,512]{1,0:T(2,128)S(1)} fusion(bf16[2,4992]{1,0:T(2,128)(2,1)S(1)} %pad_maximum_fusion.4, bf16[4992,512]{1,0:T(8,128)(2,1)} %data.11), kind=kOutput, calls=%fused_computation.104 | convolution fusion | flops 10223616 | bytes 5135872 | tf_op jit(solution)/shard_map/dot_general | solution.py:221
  43.8 1.2 collective-permute-start.22
  45.6 1.8 shard_map.67
  47.4 0.8 copy-done
  48.2 2.0 %shard_map.71 = bf16[4864,128]{1,0:T(8,128)(2,1)S(1)} custom-call(s32[4]{0:T(128)} %bitcast.44, bf16[4992,512]{1,0:T(8,128)(2,1)} %data.11), custom_call_target="tpu_custom_call" | custom-call | bytes 2490368 | tf_op jit(solution)/shard_map/pallas_call | solution.py:113
  50.2 1.8 shard_map.70
  52.0 1.8 shard_map.69
  53.8 0.9 collective-permute-start.30
  56.4 2.5 %fusion.14 = (f32[1,512]{1,0:T(1,128)S(1)}, f32[1,512]{1,0:T(1,128)S(1)}) fusion(f32[1,512]{1,0:T(1,128)S(1)} %get-tuple-element.82, f32[2,640]{1,0:T(2,128)S(1)} %add_add_fusion.2, f32[]{:T(128)S(6)} %add.175, f32[]{:T(128)} %bitcast.30, f32[]{:T(128)} %bitcast.29, f32[1,512]{1,0:T(1,128)S(1)} %get-tuple-element.80, f32[]{:T(128)S(6)} %add.173, ...), kind=kLoop, calls=%fused_computation.79 | loop fusion | flops 7168 | bytes 12312 | tf_op jit(solution)/shard_map/max | solution.py:60
  59.0 3.9 %fusion.17 = f32[2,4992]{1,0:T(2,128)S(1)} fusion(bf16[4992,512]{1,0:T(8,128)(2,1)} %data.11, f32[2,512]{1,0:T(2,128)S(1)} %pad_maximum_fusion.5), kind=kOutput, calls=%fused_computation.83 | convolution fusion | flops 10224640 | bytes 5155840 | tf_op jit(solution)/shard_map/dot_general | solution.py:225
  63.6 0.7 fusion.20
  65.7 2.9 %collective-permute-start.11 = (s32[1]{0:T(128)}, s32[1]{0:T(128)}, u32[]{:S(2)}, u32[]{:S(2)}) collective-permute-start(s32[1]{0:T(128)} %bitcast.17), channel_id=1, source_target_pairs={{0,1},{1,0},{2,3},{3,2},{4,5},{5,4},{6,7},{7,6},{8,9},{9,8},{10,11... | collective-permute-start | bytes 20 | tf_op jit(solution)/shard_map/ppermute | solution.py:19
  68.6 0.7 collective-permute-done.11
  70.0 3.4 %collective-permute-start.24 = (f32[1,5120]{1,0:T(1,128)S(1)}, f32[1,5120]{1,0:T(1,128)S(1)}, u32[]{:S(2)}, u32[]{:S(2)}) collective-permute-start(f32[1,5120]{1,0:T(1,128)S(1)} %fusion.1), channel_id=1, source_target_pairs={{0,2},{1,3},{2,0},{3,1},{4,6},{5,7},{6,4},{7,5},{8,10},{9,11},{10,... | collective-permute-start | bytes 61448 | tf_op jit(solution)/shard_map/ppermute | solution.py:19
  73.6 1.4 collective-permute-start.26
  75.0 2.5 %add_maximum_fusion.8 = (f32[4992]{0:T(1024)S(1)}, f32[4992]{0:T(1024)S(1)}) fusion(f32[4992]{0:T(1024)S(1)} %get-tuple-element.63, f32[4992]{0:T(1024)S(1)} %get-tuple-element.128, f32[]{:T(128)S(6)} %add.168, f32[]{:T(128)} %bitcast.26, f32[]{:T(128)} %bitcast.25, f32[4992]{0:T(1024)S(1)} %get-tuple-element.64, f32[]{:T(128)S(6)} %add.166, f32[]{:T(128)} %bitcast.24, ...), kind=kLoop, calls=%fused_computation.39 | loop fusion | flops 69888 | bytes 119832 | tf_op jit(solution)/shard_map/max | solution.py:60
  77.5 9.0 %collective-permute-done.24 = f32[1,5120]{1,0:T(1,128)S(1)} collective-permute-done((f32[1,5120]{1,0:T(1,128)S(1)}, f32[1,5120]{1,0:T(1,128)S(1)}, u32[]{:S(2)}, u32[]{:S(2)}) %collective-permute-start.24) | collective-permute-done | bytes 20512 | tf_op jit(solution)/shard_map/ppermute | solution.py:19
  86.6 38.6 %collective-permute-done.25 = f32[1,5120]{1,0:T(1,128)S(1)} collective-permute-done((f32[1,5120]{1,0:T(1,128)S(1)}, f32[1,5120]{1,0:T(1,128)S(1)}, u32[]{:S(2)}, u32[]{:S(2)}) %collective-permute-start.25) | collective-permute-done | bytes 20512 | tf_op jit(solution)/shard_map/ppermute | solution.py:19
  125.2 2.4 %collective-permute-done.26 = f32[1,5120]{1,0:T(1,128)S(1)} collective-permute-done((f32[1,5120]{1,0:T(1,128)S(1)}, f32[1,5120]{1,0:T(1,128)S(1)}, u32[]{:S(2)}, u32[]{:S(2)}) %collective-permute-start.26) | collective-permute-done | bytes 20512 | tf_op jit(solution)/shard_map/ppermute | solution.py:19
  127.7 38.9 %conditional.1 = (bf16[2432,128]{1,0:T(8,128)(2,1)}, bf16[2560,128]{1,0:T(8,128)(2,1)}, f32[2,4992]{1,0:T(2,128)S(1)}) conditional(s32[]{:T(128)} %clamp.3, (f32[1,5120]{1,0:T(1,128)S(1)}, f32[4992]{0:T(1024)S(1)}, f32[4992]{0:T(1024)S(1)}) %tuple.24, (bf16[2432,128]{1,0:T(8,128)(2,1)}, bf16[2560,128]{1,0:T(8,128)(2,1)}, ...), branch_computations={%region_2.3_spmd, %region_3.4_spmd, %region_4.5_spmd, %region_5.6_... | conditional | flops 90118 | bytes 5635338 | solution.py:256
  128.3 1.3 collective-permute-start.5
  129.6 2.8 %collective-permute-start.4 = (bf16[2432,128]{1,0:T(8,128)(2,1)}, bf16[2432,128]{1,0:T(8,128)(2,1)}, u32[]{:S(2)}, u32[]{:S(2)}) collective-permute-start(bf16[2432,128]{1,0:T(8,128)(2,1)} %get-tuple-element.44), channel_id=1, source_target_pairs={{1,5},{3,7},{5,1},{7,3},{9,13},{11,15},{13,9},{15,11},{17,21},{19,... | collective-permute-start | bytes 1867784 | tf_op jit(solution)/shard_map/cond/branch_2_fun/ppermute | solution.py:245
  132.5 0.7 fusion.32
  134.5 2.6 %add_maximum_fusion.4 = (f32[4992]{0:T(1024)S(1)}, f32[4992]{0:T(1024)S(1)}) fusion(f32[4992]{0:T(1024)S(1)} %get-tuple-element.48, f32[4992]{0:T(1024)S(1)} %get-tuple-element.109, f32[]{:T(128)S(6)} %add.111, f32[]{:T(128)} %bitcast.11, f32[]{:T(128)} %bitcast.10, f32[4992]{0:T(1024)S(1)} %get-tuple-element.46, f32[]{:T(128)S(6)} %add.109, f32[]{:T(128)} %bitcast.9, ...), kind=kLoop, calls=%fused_computation.17 | loop fusion | flops 69888 | bytes 119832 | tf_op jit(solution)/shard_map/cond/branch_2_fun/max | solution.py:60
  137.3 29.3 %collective-permute-done.4 = bf16[2432,128]{1,0:T(8,128)(2,1)} collective-permute-done((bf16[2432,128]{1,0:T(8,128)(2,1)}, bf16[2432,128]{1,0:T(8,128)(2,1)}, u32[]{:S(2)}, u32[]{:S(2)}) %collective-permute-start.4) | collective-permute-done | bytes 622624 | tf_op jit(solution)/shard_map/cond/branch_2_fun/ppermute | solution.py:245
  166.5 4.0 %collective-permute-start.28 = (bf16[2432,128]{1,0:T(8,128)(2,1)S(1)}, bf16[2432,128]{1,0:T(8,128)(2,1)S(1)}, u32[]{:S(2)}, u32[]{:S(2)}) collective-permute-start(bf16[2432,128]{1,0:T(8,128)(2,1)S(1)} %shard_map.69), channel_id=1, source_target_pairs={{0,4},{1,5},{2,6},{3,7},{4,0},{5,1},{6,2},{7,3},{8,12},{9,13},{10,... | collective-permute-start | bytes 1867784 | tf_op jit(solution)/shard_map/ppermute | solution.py:19
  170.6 8.5 %keep.1.refs_2_ = bf16[4992,1024]{1,0:T(8,128)(2,1)} custom-call(s32[4]{0:T(128)} %bitcast.47, bf16[4992,512]{1,0:T(8,128)(2,1)} %data.11), custom_call_target="tpu_custom_call" | custom-call | bytes 15335424 | tf_op jit(solution)/shard_map/keep/pallas_call | solution.py:134
  179.1 2.8 %shard_map.72.refs_3_ = bf16[4992,1024]{1,0:T(8,128)(2,1)} custom-call(s32[4]{0:T(128)} %copy-done.8, bf16[2688,128]{1,0:T(8,128)(2,1)} %collective-permute-done.29.refs_0_, bf16[4864,128]{1,0:T(8,128)(2,1)} %collective-permute-done.30.refs_1_, bf16[4992,1024]{1,0:T(8,128)(2,1)} %keep.1.refs_2_), custom_call_target="tpu_custom_call", output_to_operand_aliasing={{}: (3, {})} | custom-call | bytes 3866624 | tf_op jit(solution)/shard_map/pallas_call | solution.py:170
  181.9 2.3 %collective-permute-done.28.refs_0_ = bf16[2432,128]{1,0:T(8,128)(2,1)S(1)} collective-permute-done((bf16[2432,128]{1,0:T(8,128)(2,1)S(1)}, bf16[2432,128]{1,0:T(8,128)(2,1)S(1)}, u32[]{:S(2)}, u32[]{:S(2)}) %collective-permute-start.28) | collective-permute-done | bytes 622624 | tf_op jit(solution)/shard_map/ppermute | solution.py:19
  184.3 0.8 copy-done.1
  185.1 2.8 %shard_map.73 = bf16[4992,1024]{1,0:T(8,128)(2,1)} custom-call(s32[4]{0:T(128)} %copy-done.8, bf16[2432,128]{1,0:T(8,128)(2,1)} %copy-done.1, bf16[2432,128]{1,0:T(8,128)(2,1)} %get-tuple-element.61.refs_1_, bf16[2560,128]{1,0:T(8,128)(2,1)} %get-tuple-element.62.refs_2_, bf16[4992,1024]{1,0:T(8,128)(2,1)} %shard_map.72.refs_3_), custom_call_target="tpu_custom_call", output_to_operand_aliasing={{}: (4, {})} | custom-call | bytes 3801088 | tf_op jit(solution)/shard_map/pallas_call | solution.py:170
  (69 shorter events, 8.2 us)
Async XLA Ops:
  0.6 10.8 %copy-start.7 = (f32[2,512]{1,0:T(2,128)S(1)}, f32[2,512]{1,0:T(2,128)}, u32[]{:S(2)}) copy-start(f32[2,512]{1,0:T(2,128)} %param.11) | copy-start | bytes 12292
  1.6 27.9 %copy-start.4 = (s32[4,1]{0,1:T(1,128)S(1)}, s32[4,1]{0,1:T(1,128)}, u32[]{:S(2)}) copy-start(s32[4,1]{0,1:T(1,128)} %param.9) | copy-start | bytes 52
  4.9 1.9 collective-permute-start.12
  4.9 3.7 %collective-permute-start.13 = (f32[2,640]{1,0:T(2,128)S(1)}, f32[2,640]{1,0:T(2,128)S(1)}, u32[]{:S(2)}, u32[]{:S(2)}) collective-permute-start(f32[2,640]{1,0:T(2,128)S(1)} %select_maximum_fusion.3), channel_id=1, source_target_pairs={{0,16},{8,24},{16,0},{24,8},{1,17},{9,25},{17,1},{25,9},{2,18},{10... | collective-permute-start | bytes 15368 | tf_op jit(solution)/shard_map/ppermute | solution.py:19
  6.5 3.0 %collective-permute-start.14 = (f32[2,640]{1,0:T(2,128)S(1)}, f32[2,640]{1,0:T(2,128)S(1)}, u32[]{:S(2)}, u32[]{:S(2)}) collective-permute-start(f32[2,640]{1,0:T(2,128)S(1)} %select_maximum_fusion.3), channel_id=1, source_target_pairs={{0,24},{8,16},{16,8},{24,0},{1,25},{9,17},{17,9},{25,1},{2,26},{10... | collective-permute-start | bytes 15368 | tf_op jit(solution)/shard_map/ppermute | solution.py:19
  14.1 22.9 %copy-start.2 = (f32[2,4992]{1,0:T(2,128)S(1)}, f32[2,4992]{1,0:T(2,128)}, u32[]{:S(2)}) copy-start(f32[2,4992]{1,0:T(2,128)} %param.10) | copy-start | bytes 119812
  18.2 3.8 %collective-permute-start.15 = (f32[1,5120]{1,0:T(1,128)S(1)}, f32[1,5120]{1,0:T(1,128)S(1)}, u32[]{:S(2)}, u32[]{:S(2)}) collective-permute-start(f32[1,5120]{1,0:T(1,128)S(1)} %broadcast_select_fusion.12), channel_id=1, source_target_pairs={{0,1},{1,0},{2,3},{3,2},{4,5},{5,4},{6,7},{7,6},{8,9},{9,8},{10,11... | collective-permute-start | bytes 61448 | tf_op jit(solution)/shard_map/ppermute | solution.py:19
  22.0 3.8 %collective-permute-start.16 = (f32[1,5120]{1,0:T(1,128)S(1)}, f32[1,5120]{1,0:T(1,128)S(1)}, u32[]{:S(2)}, u32[]{:S(2)}) collective-permute-start(f32[1,5120]{1,0:T(1,128)S(1)} %fusion), channel_id=1, source_target_pairs={{0,2},{1,3},{2,0},{3,1},{4,6},{5,7},{6,4},{7,5},{8,10},{9,11},{10,... | collective-permute-start | bytes 61448 | tf_op jit(solution)/shard_map/ppermute | solution.py:19
  22.6 4.7 %collective-permute-start.17 = (f32[1,5120]{1,0:T(1,128)S(1)}, f32[1,5120]{1,0:T(1,128)S(1)}, u32[]{:S(2)}, u32[]{:S(2)}) collective-permute-start(f32[1,5120]{1,0:T(1,128)S(1)} %fusion), channel_id=1, source_target_pairs={{0,4},{1,5},{2,6},{3,7},{4,0},{5,1},{6,2},{7,3},{8,12},{9,13},{10,... | collective-permute-start | bytes 61448 | tf_op jit(solution)/shard_map/ppermute | solution.py:19
  25.2 3.8 %collective-permute-start.18 = (f32[1,5120]{1,0:T(1,128)S(1)}, f32[1,5120]{1,0:T(1,128)S(1)}, u32[]{:S(2)}, u32[]{:S(2)}) collective-permute-start(f32[1,5120]{1,0:T(1,128)S(1)} %fusion), channel_id=1, source_target_pairs={{0,6},{1,7},{2,4},{3,5},{4,2},{5,3},{6,0},{7,1},{8,14},{9,15},{10,... | collective-permute-start | bytes 61448 | tf_op jit(solution)/shard_map/ppermute | solution.py:19
  29.0 6.1 %collective-permute-start.19 = (f32[1,5120]{1,0:T(1,128)S(1)}, f32[1,5120]{1,0:T(1,128)S(1)}, u32[]{:S(2)}, u32[]{:S(2)}) collective-permute-start(f32[1,5120]{1,0:T(1,128)S(1)} %add_add_fusion.1), channel_id=1, source_target_pairs={{0,1},{1,0},{2,3},{3,2},{4,5},{5,4},{6,7},{7,6},{8,9},{9,8},{10,11... | collective-permute-start | bytes 61448 | tf_op jit(solution)/shard_map/ppermute | solution.py:19
  29.6 15.4 %copy-start.5 = (s32[4,1]{0,1:T(1,128)S(1)}, s32[4,1]{0,1:T(1,128)}, u32[]{:S(2)}) copy-start(s32[4,1]{0,1:T(1,128)} %param.9) | copy-start | bytes 52
  29.6 34.1 %collective-permute-start.10 = (s32[4]{0:T(128)S(1)}, s32[4]{0:T(128)S(1)}, u32[]{:S(2)}, u32[]{:S(2)}) collective-permute-start(s32[4]{0:T(128)S(1)} %bitcast.48), channel_id=1, source_target_pairs={{0,4},{1,5},{2,6},{3,7},{4,0},{5,1},{6,2},{7,3},{8,12},{9,13},{10,... | collective-permute-start | bytes 56 | tf_op jit(solution)/shard_map/ppermute | solution.py:19
  33.5 94.2 %collective-permute-start.27 = (bf16[2560,128]{1,0:T(8,128)(2,1)S(1)}, bf16[2560,128]{1,0:T(8,128)(2,1)}, u32[]{:S(2)}, u32[]{:S(2)}) collective-permute-start(bf16[2560,128]{1,0:T(8,128)(2,1)S(1)} %shard_map.68), channel_id=1, source_target_pairs={{0,1},{1,0},{2,3},{3,2},{4,5},{5,4},{6,7},{7,6},{8,9},{9,8},{10,11... | collective-permute-start | bytes 1966088 | tf_op jit(solution)/shard_map/ppermute | solution.py:19
  43.1 10.7 %collective-permute-start.20 = (f32[2,640]{1,0:T(2,128)S(1)}, f32[2,640]{1,0:T(2,128)S(1)}, u32[]{:S(2)}, u32[]{:S(2)}) collective-permute-start(f32[2,640]{1,0:T(2,128)S(1)} %select_maximum_fusion.2), channel_id=1, source_target_pairs={{0,8},{8,0},{16,24},{24,16},{1,9},{9,1},{17,25},{25,17},{2,10},{10... | collective-permute-start | bytes 15368 | tf_op jit(solution)/shard_map/ppermute | solution.py:19
  43.1 11.5 %collective-permute-start.21 = (f32[2,640]{1,0:T(2,128)S(1)}, f32[2,640]{1,0:T(2,128)S(1)}, u32[]{:S(2)}, u32[]{:S(2)}) collective-permute-start(f32[2,640]{1,0:T(2,128)S(1)} %select_maximum_fusion.2), channel_id=1, source_target_pairs={{0,16},{8,24},{16,0},{24,8},{1,17},{9,25},{17,1},{25,9},{2,18},{10... | collective-permute-start | bytes 15368 | tf_op jit(solution)/shard_map/ppermute | solution.py:19
  43.8 10.9 %collective-permute-start.22 = (f32[2,640]{1,0:T(2,128)S(1)}, f32[2,640]{1,0:T(2,128)S(1)}, u32[]{:S(2)}, u32[]{:S(2)}) collective-permute-start(f32[2,640]{1,0:T(2,128)S(1)} %select_maximum_fusion.2), channel_id=1, source_target_pairs={{0,24},{8,16},{16,8},{24,0},{1,25},{9,17},{17,9},{25,1},{2,26},{10... | collective-permute-start | bytes 15368 | tf_op jit(solution)/shard_map/ppermute | solution.py:19
  47.4 0.8 copy-start
  53.8 125.3 %collective-permute-start.30 = (bf16[4864,128]{1,0:T(8,128)(2,1)S(1)}, bf16[4864,128]{1,0:T(8,128)(2,1)}, u32[]{:S(2)}, u32[]{:S(2)}) collective-permute-start(bf16[4864,128]{1,0:T(8,128)(2,1)S(1)} %shard_map.71), channel_id=1, source_target_pairs={{0,4},{1,5},{2,6},{3,7},{4,0},{5,1},{6,2},{7,3},{8,12},{9,13},{10,... | collective-permute-start | bytes 3735560 | tf_op jit(solution)/shard_map/ppermute | solution.py:19
  59.0 120.1 %copy-start.6 = (f32[2,512]{1,0:T(2,128)}, f32[2,512]{1,0:T(2,128)S(1)}, u32[]{:S(2)}) copy-start(f32[2,512]{1,0:T(2,128)S(1)} %pad_maximum_fusion.5) | copy-start | bytes 12292
  63.1 6.9 %collective-permute-start.23 = (f32[1,5120]{1,0:T(1,128)S(1)}, f32[1,5120]{1,0:T(1,128)S(1)}, u32[]{:S(2)}, u32[]{:S(2)}) collective-permute-start(f32[1,5120]{1,0:T(1,128)S(1)} %broadcast_select_fusion.8), channel_id=1, source_target_pairs={{0,1},{1,0},{2,3},{3,2},{4,5},{5,4},{6,7},{7,6},{8,9},{9,8},{10,11... | collective-permute-start | bytes 61448 | tf_op jit(solution)/shard_map/ppermute | solution.py:19
  63.6 115.4 %copy-start.8 = (s32[4]{0:T(128)}, s32[4]{0:T(128)S(1)}, u32[]{:S(2)}) copy-start(s32[4]{0:T(128)S(1)} %collective-permute-done.10.labels) | copy-start | bytes 52
  65.7 3.6 %collective-permute-start.11 = (s32[1]{0:T(128)}, s32[1]{0:T(128)}, u32[]{:S(2)}, u32[]{:S(2)}) collective-permute-start(s32[1]{0:T(128)} %bitcast.17), channel_id=1, source_target_pairs={{0,1},{1,0},{2,3},{3,2},{4,5},{5,4},{6,7},{7,6},{8,9},{9,8},{10,11... | collective-permute-start | bytes 20 | tf_op jit(solution)/shard_map/ppermute | solution.py:19
  70.0 16.5 %collective-permute-start.24 = (f32[1,5120]{1,0:T(1,128)S(1)}, f32[1,5120]{1,0:T(1,128)S(1)}, u32[]{:S(2)}, u32[]{:S(2)}) collective-permute-start(f32[1,5120]{1,0:T(1,128)S(1)} %fusion.1), channel_id=1, source_target_pairs={{0,2},{1,3},{2,0},{3,1},{4,6},{5,7},{6,4},{7,5},{8,10},{9,11},{10,... | collective-permute-start | bytes 61448 | tf_op jit(solution)/shard_map/ppermute | solution.py:19
  73.5 51.7 %collective-permute-start.25 = (f32[1,5120]{1,0:T(1,128)S(1)}, f32[1,5120]{1,0:T(1,128)S(1)}, u32[]{:S(2)}, u32[]{:S(2)}) collective-permute-start(f32[1,5120]{1,0:T(1,128)S(1)} %fusion.1), channel_id=1, source_target_pairs={{0,4},{1,5},{2,6},{3,7},{4,0},{5,1},{6,2},{7,3},{8,12},{9,13},{10,... | collective-permute-start | bytes 61448 | tf_op jit(solution)/shard_map/ppermute | solution.py:19
  73.6 54.0 %collective-permute-start.26 = (f32[1,5120]{1,0:T(1,128)S(1)}, f32[1,5120]{1,0:T(1,128)S(1)}, u32[]{:S(2)}, u32[]{:S(2)}) collective-permute-start(f32[1,5120]{1,0:T(1,128)S(1)} %fusion.1), channel_id=1, source_target_pairs={{0,6},{1,7},{2,4},{3,5},{4,2},{5,3},{6,0},{7,1},{8,14},{9,15},{10,... | collective-permute-start | bytes 61448 | tf_op jit(solution)/shard_map/ppermute | solution.py:19
  86.6 92.5 %collective-permute-start.29 = (bf16[2688,128]{1,0:T(8,128)(2,1)S(1)}, bf16[2688,128]{1,0:T(8,128)(2,1)}, u32[]{:S(2)}, u32[]{:S(2)}) collective-permute-start(bf16[2688,128]{1,0:T(8,128)(2,1)S(1)} %shard_map.70), channel_id=1, source_target_pairs={{0,4},{1,5},{2,6},{3,7},{4,0},{5,1},{6,2},{7,3},{8,12},{9,13},{10,... | collective-permute-start | bytes 2064392 | tf_op jit(solution)/shard_map/ppermute | solution.py:19
  127.7 4.7 %collective-permute-start.6 = (f32[1,5120]{1,0:T(1,128)S(1)}, f32[1,5120]{1,0:T(1,128)S(1)}, u32[]{:S(2)}, u32[]{:S(2)}) collective-permute-start(f32[1,5120]{1,0:T(1,128)S(1)} %get-tuple-element.47), channel_id=1, source_target_pairs={{0,1},{1,0},{2,3},{3,2},{4,5},{5,4},{6,7},{7,6},{8,9},{9,8},{10,11... | collective-permute-start | bytes 61448 | tf_op jit(solution)/shard_map/cond/branch_2_fun/ppermute | solution.py:19
  128.3 38.3 %collective-permute-start.5 = (bf16[2560,128]{1,0:T(8,128)(2,1)}, bf16[2560,128]{1,0:T(8,128)(2,1)}, u32[]{:S(2)}, u32[]{:S(2)}) collective-permute-start(bf16[2560,128]{1,0:T(8,128)(2,1)} %get-tuple-element.45), channel_id=1, source_target_pairs={{0,5},{2,7},{4,1},{6,3},{8,13},{10,15},{12,9},{14,11},{16,21},{18,... | collective-permute-start | bytes 1966088 | tf_op jit(solution)/shard_map/cond/branch_2_fun/ppermute | solution.py:246
  129.6 37.0 %collective-permute-start.4 = (bf16[2432,128]{1,0:T(8,128)(2,1)}, bf16[2432,128]{1,0:T(8,128)(2,1)}, u32[]{:S(2)}, u32[]{:S(2)}) collective-permute-start(bf16[2432,128]{1,0:T(8,128)(2,1)} %get-tuple-element.44), channel_id=1, source_target_pairs={{1,5},{3,7},{5,1},{7,3},{9,13},{11,15},{13,9},{15,11},{17,21},{19,... | collective-permute-start | bytes 1867784 | tf_op jit(solution)/shard_map/cond/branch_2_fun/ppermute | solution.py:245
  166.5 12.5 %copy-start.3 = (f32[2,4992]{1,0:T(2,128)}, f32[2,4992]{1,0:T(2,128)S(1)}, u32[]{:S(2)}) copy-start(f32[2,4992]{1,0:T(2,128)S(1)} %get-tuple-element.57) | copy-start | bytes 119812
  166.5 17.7 %collective-permute-start.28 = (bf16[2432,128]{1,0:T(8,128)(2,1)S(1)}, bf16[2432,128]{1,0:T(8,128)(2,1)S(1)}, u32[]{:S(2)}, u32[]{:S(2)}) collective-permute-start(bf16[2432,128]{1,0:T(8,128)(2,1)S(1)} %shard_map.69), channel_id=1, source_target_pairs={{0,4},{1,5},{2,6},{3,7},{4,0},{5,1},{6,2},{7,3},{8,12},{9,13},{10,... | collective-permute-start | bytes 1867784 | tf_op jit(solution)/shard_map/ppermute | solution.py:19
  184.2 0.8 copy-start.1
